TPU v7x, 32 devices: a whole 2x2x4 slice. The times are simulated.
32 devices in a mesh: chan: 4 (over y, x), hid: 8 (over z, core).
Axes of the slice: x: 2, y: 2, z: 4, core: 2. Of those that a mesh axis runs over, the one named last changes fastest.
Arguments:
- pixels: bfloat16 [384, 256, 256], P('chan'), may hold values from -6 to 6
- patch_weight: bfloat16 [384, 256, 6144], P('chan', None, 'hid'), may hold values from -0.375 to 0.375
- channel_embed: bfloat16 [384, 6144], P('chan', 'hid'), may hold values from -3 to 3
- pool_query: bfloat16 [48, 6144], P('chan', 'hid'), may hold values from -2.5 to 2.5
- group_mix: bfloat16 [48, 6144], P('chan', 'hid'), may hold values from -3.2 to 3.2
- assign: int32 [384], P('chan'), may hold values from 0 to 47, as said below
- ln_gain: float32 [6144], P('chan'), may hold values from 0.1 to 1.9
- w_qkv: bfloat16 [6144, 3, 6144], P('chan', None, 'hid'), may hold values from -0.078125 to 0.078125
- w_up: bfloat16 [6144, 24576], P('chan', 'hid'), may hold values from -0.078125 to 0.078125
- b_up: float32 [24576], P('hid'), may hold values from -3 to 3
- w_out: bfloat16 [6144, 6144], P('hid', 'chan'), may hold values from -0.078125 to 0.078125
- w_down: bfloat16 [24576, 6144], P('hid', 'chan'), may hold values from -0.0390625 to 0.0390625
Outputs:
- block_out: bfloat16 [256, 6144], P(None, 'chan')
Inputs may be any that keep to these rules, and one draw needn't show every extreme that they name: Channel c belongs to group assign[c]; every group holds exactly 8 channels, and group k's channels all lie among the 96 consecutive channels beginning at channel (k // 12) * 96.
All inputs are finite; a program needn't handle non-finite values.
Results may differ from a plain program's by a relative error of at most 0.02.
Values may be sent and summed in bfloat16 or wider, within the bound.
A program may use at most 320 MiB of HBM per device.

v0:
```python
import functools
import math

import jax
import jax.numpy as jnp
from jax import lax
from jax.experimental import pallas as pl
from jax.experimental.pallas import tpu as pltpu
from jax.sharding import PartitionSpec as P

HS = 128
PATCHES = 256


epsilon = 1e-06


def pool_kernel(size, order_ref, pix_ref, pw_ref, emb_ref, query_ref, shift_ref, mix_ref, out_ref, feat, sq, numer, denom, acc, pick, quer):
    g = pl.program_id(0); j = pl.program_id(1)
    tok, width = acc.shape
    heads = width // HS
    head = lax.broadcasted_iota(jnp.int32, (HS, width), 0)
    head_of = lax.broadcasted_iota(jnp.int32, (HS, width), 1) // HS

    @pl.when((g == 0) & (j == 0))
    def _():
        acc[...] = jnp.zeros_like(acc)
        pick[...] = jnp.where(head_of == head, 1.0, 0.0).astype(jnp.bfloat16)

    @pl.when(j == 0)
    def _():
        quer[...] = jnp.where(head_of == head, query_ref[0], 0.0).astype(jnp.bfloat16)

    across = (((1,), (1,)), ((), ()))
    step = min(256, width)
    for n in range(width // step):
        cs = slice(n * step, (n + 1) * step)
        for r in range(0, tok, 64):
            e = jnp.dot(pix_ref[0, r:r+64], pw_ref[0, :, cs], preferred_element_type=jnp.float32)
            e = e + emb_ref[0, :, cs]
            f = (0.5 * e) * (1.0 + lax.erf(e * math.sqrt(0.5)))
            feat[r:r+64, cs] = f.astype(jnp.bfloat16)
            sq[r:r+64, cs] = (f * f).astype(jnp.bfloat16)
    dots = lax.dot_general(feat[...], quer[...], across, preferred_element_type=jnp.float32)
    total = lax.dot_general(sq[...], pick[...], across, preferred_element_type=jnp.float32)
    score = dots * lax.rsqrt(total * (1.0 / HS) + epsilon) * (1.0 / math.sqrt(HS))
    weight = jnp.exp(score - shift_ref[0])
    @pl.when(j == 0)
    def _():
        denom[...] = weight
        for h in range(heads):
            hs = slice(h * HS, (h + 1) * HS)
            numer[:, hs] = weight[:, h:h+1] * feat[:, hs].astype(jnp.float32)
    @pl.when(j > 0)
    def _():
        denom[...] += weight
        for h in range(heads):
            hs = slice(h * HS, (h + 1) * HS)
            numer[:, hs] += weight[:, h:h+1] * feat[:, hs].astype(jnp.float32)
    @pl.when(j == size - 1)
    def _():
        inv = 1.0 / denom[...]
        for h in range(heads):
            hs = slice(h * HS, (h + 1) * HS)
            acc[:, hs] += numer[:, hs] * inv[:, h:h+1] * mix_ref[0, :, hs]
    @pl.when((g == pl.num_programs(0) - 1) & (j == size - 1))
    def _():
        out_ref[...] = acc[...].astype(jnp.bfloat16)

def pool(pixels, patch_weight, channel_embed, pool_query, group_mix, assign):
    chans, tok, p2 = pixels.shape
    width = patch_weight.shape[2]
    groups = pool_query.shape[0]
    size = chans // groups
    heads = width // HS
    idx = jnp.arange(chans, dtype=jnp.int32)
    key = assign * chans + idx
    rank = jnp.sum((key[None, :] < key[:, None]).astype(jnp.int32), axis=1)
    order = jnp.sum(jnp.where(rank[None, :] == idx[:, None], idx[None, :], 0), axis=1).astype(jnp.int32)
    q = pool_query.astype(jnp.float32)
    sh = jnp.sqrt(jnp.sum((q * q).reshape(groups, heads, HS), axis=-1))
    sh = jnp.pad(sh, ((0, 0), (0, HS - heads))).reshape(groups, 1, HS)
    spec = pltpu.PrefetchScalarGridSpec(
        num_scalar_prefetch=1, grid=(groups, size),
        in_specs=[
            pl.BlockSpec((1, tok, p2), lambda g, j, o: (o[g * size + j], 0, 0)),
            pl.BlockSpec((1, p2, width), lambda g, j, o: (o[g * size + j], 0, 0)),
            pl.BlockSpec((1, 1, width), lambda g, j, o: (o[g * size + j], 0, 0)),
            pl.BlockSpec((1, 1, width), lambda g, j, o: (g, 0, 0)),
            pl.BlockSpec((1, 1, HS), lambda g, j, o: (g, 0, 0)),
            pl.BlockSpec((1, 1, width), lambda g, j, o: (g, 0, 0)),
        ],
        out_specs=pl.BlockSpec((tok, width), lambda g, j, o: (0, 0)),
        scratch_shapes=[
            pltpu.VMEM((tok, width), jnp.bfloat16), pltpu.VMEM((tok, width), jnp.bfloat16),
            pltpu.VMEM((tok, width), jnp.float32), pltpu.VMEM((tok, HS), jnp.float32),
            pltpu.VMEM((tok, width), jnp.float32), pltpu.VMEM((HS, width), jnp.bfloat16), pltpu.VMEM((HS, width), jnp.bfloat16)])
    return pl.pallas_call(
        functools.partial(pool_kernel, size), grid_spec=spec,
        out_shape=jax.ShapeDtypeStruct((tok, width), jnp.bfloat16),
        compiler_params=pltpu.CompilerParams(dimension_semantics=("arbitrary", "arbitrary"), vmem_limit_bytes=40 << 20),
        name="pool",
    )(order, pixels, patch_weight, channel_embed.astype(jnp.float32).reshape(chans, 1, width), q.reshape(groups, 1, width), sh,
      group_mix.astype(jnp.float32).reshape(groups, 1, width))


def head_norm(values):
    return values * lax.rsqrt(jnp.mean(values * values, axis=-1, keepdims=True) + epsilon)


MESH = pl.DeviceIdType.MESH


def greet(peers):
    gate = pltpu.get_barrier_semaphore()
    for peer in peers:
        pl.semaphore_signal(gate, inc=1, device_id=peer, device_id_type=MESH)
    pl.semaphore_wait(gate, len(peers))


def send(src, dst, sems, slot, peer):
    copy = pltpu.make_async_remote_copy(
        src_ref=src, dst_ref=dst, send_sem=sems.at[0, slot], recv_sem=sems.at[1, slot],
        device_id=peer, device_id_type=MESH)
    copy.start()
    return copy


def places(chans, hids):
    a, b = lax.axis_index("chan"), lax.axis_index("hid")
    chips, chip, core = hids // 2, b // 2, b % 2
    rows = [{"chan": lax.rem(a + k, chans)} for k in range(1, chans)]
    far = [{"hid": lax.rem(chip + k, chips) * 2 + core} for k in range(1, chips)]
    return a, b, chips, chip, core, rows, far, {"hid": chip * 2 + (1 - core)}


def spread(src_of, slots, chips, chip, core, far, mate, away, near):
    sent = [send(src_of(chip * 2 + core), src_of(chip * 2 + core), away, k, peer) for k, peer in enumerate(far)]
    mine = src_of(chip * 2 + core)
    passed = [send(mine, mine, near, 0, mate)]
    for k in range(1, chips):
        sent[k - 1].wait_recv()
        piece = src_of(lax.rem(chip + chips - k, chips) * 2 + core)
        passed.append(send(piece, piece, near, k, mate))
    for copy in passed:
        copy.wait()
    for copy in sent:
        copy.wait_send()


def layer_kernel(chans, hids, part, gain, normed_ref, own_ref, parts, gath, stat, whole, stats, s1, s2, s3, s4, s5):
    a, b, chips, chip, core, rows, far, mate = places(chans, hids)
    greet(rows + far + [mate])
    width = part.shape[2]
    size = part.shape[1]
    copies = [send(part.at[lax.rem(a + k, chans)], parts.at[k - 1], s1, k - 1, rows[k - 1]) for k in range(1, chans)]
    total = part[a].astype(jnp.float32)
    for k in range(chans - 1):
        copies[k].wait_recv()
        total = total + parts[k].astype(jnp.float32)
    gath[b] = total.astype(jnp.bfloat16)
    spread(lambda i: gath.at[i], None, chips, chip, core, far, mate, s2, s3)
    first = jnp.zeros((size, 1), jnp.float32)
    second = jnp.zeros((size, 1), jnp.float32)
    for i in range(hids):
        x = gath[i].astype(jnp.float32)
        first = first + jnp.sum(x, axis=1, keepdims=True)
        second = second + jnp.sum(x * x, axis=1, keepdims=True)
    mean = first / (width * hids)
    scale = lax.rsqrt(second / (width * hids) - mean * mean + epsilon)
    stat[...] = jnp.where(lax.broadcasted_iota(jnp.int32, stat.shape, 1) == 0, mean, scale)
    ratio = hids // chans
    moved = []
    for k in range(1, chans):
        to = lax.rem(a + k, chans)
        moved.append(send(stat, stats.at[a], s5, k - 1, rows[k - 1]))
        moved.append(send(gath.at[pl.ds(to * ratio, ratio)], whole.at[a], s4, k - 1, rows[k - 1]))
    for copy in copies:
        copy.wait_send()

    def emit(i, x_of, st):
        for r in range(ratio):
            cs = slice(r * width, (r + 1) * width)
            x = x_of(r)
            own_ref[i, :, cs] = x
            normed_ref[i, :, cs] = (
                (x.astype(jnp.float32) - st[:, 0:1]) * st[:, 1:2] * gain[:, cs]
            ).astype(jnp.bfloat16)

    emit(a, lambda r: gath[a * ratio + r], stat[...])
    for copy in moved:
        copy.wait()
    for k in range(1, chans):
        i = lax.rem(a + k, chans)
        emit(i, lambda r: whole[i, r], stats[i])


def layer_rows(partial, gain, chans, hids):
    tok, width = partial.shape
    size = tok // chans
    wide = gain.shape[0]
    vm = pl.BlockSpec(memory_space=pltpu.VMEM)
    dma = pltpu.SemaphoreType.DMA
    shape = jax.ShapeDtypeStruct((chans, size, wide), jnp.bfloat16)
    normed, own = pl.pallas_call(
        functools.partial(layer_kernel, chans, hids), out_shape=(shape, shape), in_specs=[vm, vm], out_specs=(vm, vm),
        scratch_shapes=[
            pltpu.VMEM((chans - 1, size, width), jnp.bfloat16), pltpu.VMEM((hids, size, width), jnp.bfloat16),
            pltpu.VMEM((size, HS), jnp.float32), pltpu.VMEM((chans, hids // chans, size, width), jnp.bfloat16),
            pltpu.VMEM((chans, size, HS), jnp.float32),
            dma((2, chans - 1)), dma((2, hids // 2 - 1)), dma((2, hids // 2)), dma((2, chans - 1)), dma((2, chans - 1))],
        compiler_params=pltpu.CompilerParams(collective_id=1, has_side_effects=True, vmem_limit_bytes=40 << 20),
        name="layer_rows",
    )(partial.reshape(chans, size, width), gain.reshape(1, wide))
    return normed.reshape(tok, wide), own.reshape(tok, wide)


def finish_kernel(chans, hids, heads, qkv, up, bias, qkv_out, hid_out, qkv_in, up_in, s1, s2, s3, s4):
    a, rows = lax.axis_index("chan"), [{"chan": lax.rem(lax.axis_index("chan") + k, chans)} for k in range(1, chans)]
    greet(rows)
    got_q = [send(qkv.at[:, lax.rem(a + k, chans)], qkv_in.at[k - 1], s1, k - 1, rows[k - 1]) for k in range(1, chans)]
    got_u = [send(up.at[lax.rem(a + k, chans)], up_in.at[k - 1], s2, k - 1, rows[k - 1]) for k in range(1, chans)]
    for copy in got_q:
        copy.wait_recv()
    for h in range(3 * heads):
        kind, hs = h // heads, slice(h % heads * HS, (h % heads + 1) * HS)
        x = qkv[kind, a, :, hs].astype(jnp.float32)
        for k in range(chans - 1):
            x = x + qkv_in[k, kind, :, hs].astype(jnp.float32)
        if h < 2 * heads:
            x = x * lax.rsqrt(jnp.mean(x * x, axis=-1, keepdims=True) + epsilon)
        qkv_out[h, a] = x.astype(jnp.bfloat16)
    put_q = [send(qkv_out.at[:, a], qkv_out.at[:, a], s3, k, peer) for k, peer in enumerate(rows)]
    for copy in got_u:
        copy.wait_recv()
    step = HS
    for n in range(up.shape[2] // step):
        cs = slice(n * step, (n + 1) * step)
        x = up[a, :, cs].astype(jnp.float32)
        for k in range(chans - 1):
            x = x + up_in[k, :, cs].astype(jnp.float32)
        x = x + bias[:, cs]
        hid_out[a, :, cs] = ((0.5 * x) * (1.0 + lax.erf(x * math.sqrt(0.5)))).astype(jnp.bfloat16)
    put_u = [send(hid_out.at[a], hid_out.at[a], s4, k, peer) for k, peer in enumerate(rows)]
    for copy in got_q + got_u:
        copy.wait_send()
    for copy in put_q + put_u:
        copy.wait()


def finish(qkv, up, bias, heads, chans, hids):
    tok, wide = qkv.shape[1:]
    size, units = tok // chans, up.shape[1]
    vm = pl.BlockSpec(memory_space=pltpu.VMEM)
    dma = pltpu.SemaphoreType.DMA
    q, u = pl.pallas_call(
        functools.partial(finish_kernel, chans, hids, heads),
        out_shape=(jax.ShapeDtypeStruct((3 * heads, chans, size, HS), jnp.bfloat16), jax.ShapeDtypeStruct((chans, size, units), jnp.bfloat16)),
        in_specs=[vm] * 3, out_specs=(vm, vm),
        scratch_shapes=[
            pltpu.VMEM((chans - 1, 3, size, wide), jnp.bfloat16), pltpu.VMEM((chans - 1, size, units), jnp.bfloat16)]
        + [dma((2, chans - 1))] * 4,
        compiler_params=pltpu.CompilerParams(collective_id=2, has_side_effects=True, vmem_limit_bytes=40 << 20),
        name="finish",
    )(qkv.reshape(3, chans, size, wide), up.reshape(chans, size, units), bias.reshape(1, units))
    return q.reshape(3, heads, tok, HS), u.reshape(tok, units)


def total_kernel(hids, term, own, out, pair, half, pieces, s1, s2, s3, s4):
    b = lax.axis_index("hid")
    chips, chip, core = hids // 2, b // 2, b % 2
    far = [{"hid": lax.rem(chip + k, chips) * 2 + core} for k in range(1, chips)]
    mate = {"hid": chip * 2 + (1 - core)}
    greet(far + [mate])
    across = send(term.at[1 - core], pair, s1, 0, mate)
    across.wait_recv()
    for i in range(chips):
        half[i] = (term[core, i].astype(jnp.float32) + pair[i].astype(jnp.float32)).astype(jnp.bfloat16)
    copies = [send(half.at[lax.rem(chip + k, chips)], pieces.at[k - 1], s2, k - 1, far[k - 1]) for k in range(1, chips)]
    value = half[chip].astype(jnp.float32)
    for k in range(chips - 1):
        copies[k].wait_recv()
        value = value + pieces[k].astype(jnp.float32)
    out[core, chip] = (value + own[core, chip].astype(jnp.float32)).astype(jnp.bfloat16)
    spread(lambda i: out.at[i % 2, i // 2], None, chips, chip, core, far, mate, s3, s4)
    across.wait_send()
    for copy in copies:
        copy.wait_send()


def total(term, own, hids):
    tok, wide = term.shape
    chips, size = hids // 2, tok // hids
    vm = pl.BlockSpec(memory_space=pltpu.VMEM)
    dma = pltpu.SemaphoreType.DMA
    out = pl.pallas_call(
        functools.partial(total_kernel, hids),
        out_shape=jax.ShapeDtypeStruct((2, chips, size, wide), jnp.bfloat16), in_specs=[vm] * 2, out_specs=vm,
        scratch_shapes=[
            pltpu.VMEM((chips, size, wide), jnp.bfloat16), pltpu.VMEM((chips, size, wide), jnp.bfloat16),
            pltpu.VMEM((chips - 1, size, wide), jnp.bfloat16),
            dma((2, 1)), dma((2, chips - 1)), dma((2, chips - 1)), dma((2, chips))],
        compiler_params=pltpu.CompilerParams(collective_id=3, has_side_effects=True, vmem_limit_bytes=40 << 20),
        name="total",
    )(term.reshape(2, chips, size, wide), own.reshape(2, chips, size, wide))
    return out.reshape(tok, wide)


def on_device(
    chans,
    hids,
    pixels,
    patch_weight,
    channel_embed,
    pool_query,
    group_mix,
    assign,
    ln_gain,
    w_qkv,
    w_up,
    b_up,
    w_out,
    w_down,
):
    tok_count = pixels.shape[1]
    width_hid = patch_weight.shape[2]
    heads_dev = width_hid // HS
    partial_value = pool(pixels, patch_weight, channel_embed, pool_query, group_mix, assign)
    normed_input, own_cols = layer_rows(partial_value, ln_gain, chans, hids)
    qkv_part = jnp.einsum("td,dke->kte", normed_input, w_qkv, preferred_element_type=jnp.float32)
    up_part = jnp.dot(normed_input, w_up, preferred_element_type=jnp.float32)
    qkv_rows, hidden = finish(
        qkv_part.astype(jnp.bfloat16), up_part.astype(jnp.bfloat16), b_up, heads_dev, chans, hids
    )
    images = tok_count // PATCHES
    queries, keys, values = qkv_rows.reshape(3, heads_dev, images, PATCHES, HS)
    scores = jnp.einsum("hbqe,hbke->hbqk", queries, keys, preferred_element_type=jnp.float32) * (
        2.0 / math.sqrt(HS)
    )
    expo = jnp.exp(scores)
    probs = (expo / jnp.sum(expo, axis=-1, keepdims=True)).astype(jnp.bfloat16)
    attended = jnp.einsum("hbqk,hbke->bqhe", probs, values, preferred_element_type=jnp.float32)
    attended = attended.astype(jnp.bfloat16).reshape(tok_count, width_hid)
    term = jnp.dot(attended, w_out, preferred_element_type=jnp.float32) + jnp.dot(
        hidden, w_down, preferred_element_type=jnp.float32
    )
    term = term.astype(jnp.bfloat16)
    if tok_count % (16 * hids) == 0:
        return total(term, own_cols, hids)
    mixed = lax.psum(term, "hid").astype(jnp.float32)
    return (own_cols.astype(jnp.float32) + mixed).astype(jnp.bfloat16)


def solution(mesh):
    in_specs = (
        P("chan", None, None),
        P("chan", None, "hid"),
        P("chan", "hid"),
        P("chan", "hid"),
        P("chan", "hid"),
        P("chan"),
        P("chan"),
        P("chan", None, "hid"),
        P("chan", "hid"),
        P("hid"),
        P("hid", "chan"),
        P("hid", "chan"),
    )
    out_specs = P(None, "chan")
    chans, hids = mesh.shape["chan"], mesh.shape["hid"]
    return jax.shard_map(
        functools.partial(on_device, chans, hids), mesh=mesh, in_specs=in_specs, out_specs=out_specs, check_vma=False
    )
```

profile of v0, /device:TPU:25, one launch (start us, length us, event | category | flops | bytes accessed | tf_op | source)
XLA Modules:
  0.0 248.1 jit_solution(7938500509415753155)
XLA Ops:
  0.0 0.0 copy-start
  0.0 0.8 iota_add_fusion
  0.8 0.2 convert_reduce_fusion
  1.0 0.1 select_reduce_fusion.order_ref
  1.1 0.7 reshape.92.gain
  1.8 0.8 reshape.107.mix_ref
  2.6 0.8 reshape.86.query_ref
  3.3 0.7 convert_multiply_fusion
  4.1 0.1 reduce_sum.38
  4.2 1.1 reshape.105.emb_ref
  5.3 0.0 copy-start.1
  5.3 4.6 %copy-done.1 = bf16[96,256,256]{2,1,0:T(8,128)(2,1)S(1)} copy-done((bf16[96,256,256]{2,1,0:T(8,128)(2,1)S(1)}, bf16[96,256,256]{2,1,0:T(8,128)(2,1)}, u32[]{:S(2)}) %copy-start.1) | copy-done | bytes 12582936
  9.9 0.0 copy-start.4
  9.9 99.9 %pool.1 = bf16[256,768]{1,0:T(8,128)(2,1)S(1)} custom-call(s32[96]{0:T(128)S(1)} %select_reduce_fusion.order_ref, bf16[96,256,256]{2,1,0:T(8,128)(2,1)S(1)} %copy-done.1, bf16[96,256,768]{2,1,0:T(8,128)(2,1)} %pw_ref.1, f32[96,1,768]{2,1,0:T(1,128)S(1)} %reshape.105.emb_ref, f32[12,1,768]{2,1,0:T(1,128)S(1)} %reshape.86.query_ref, ...), custom_call_target="tpu_custom_call" | custom-call | tf_op jit(solution)/shard_map/pool/pallas_call | solution.py:98
  109.8 31.7 %layer_rows.1 = (bf16[4,64,1536]{2,1,0:T(8,128)(2,1)S(1)}, bf16[4,64,1536]{2,1,0:T(8,128)(2,1)S(1)}) custom-call(bf16[4,64,768]{2,1,0:T(8,128)(2,1)S(1)} %bitcast.35, f32[1,1536]{1,0:T(1,128)S(1)} %reshape.92.gain), custom_call_target="tpu_custom_call" | custom-call | tf_op jit(solution)/shard_map/layer_rows/pallas_call | solution.py:205
  141.5 0.0 copy-done.4
  141.6 0.0 copy-start.3
  141.6 0.0 slice-start
  141.6 0.0 slice-start.1
  141.6 2.0 convolution_convert_fusion.1
  143.6 1.6 copy-done.3
  145.2 0.0 copy-start.2
  145.2 0.0 slice-start.2
  145.2 2.6 %convolution_convert_fusion = bf16[256,3072]{1,0:T(8,128)(2,1)S(1)} fusion(bf16[256,1536]{1,0:T(8,128)(2,1)S(1)} %bitcast.42, bf16[1536,3072]{1,0:T(8,128)(2,1)S(1)} %copy-done.3), kind=kOutput, calls=%fused_computation | convolution fusion | flops 2416705536 | bytes 11796480 | tf_op jit(solution)/shard_map/dot_general | solution.py:331
  147.9 0.0 copy-done.2
  147.9 62.9 %finish.1 = (bf16[18,4,64,128]{3,2,1,0:T(8,128)(2,1)S(1)}, bf16[4,64,3072]{2,1,0:T(8,128)(2,1)S(1)}) custom-call(bf16[3,4,64,768]{3,2,1,0:T(8,128)(2,1)S(1)} %bitcast.37, bf16[4,64,3072]{2,1,0:T(8,128)(2,1)S(1)} %bitcast.36, f32[1,3072]{1,0:T(1,128)S(1)} %bitcast.39), custom_call_target="tpu_custom_call" | custom-call | tf_op jit(solution)/shard_map/finish/pallas_call | solution.py:256
  210.8 0.0 slice-done
  210.8 0.0 slice-done.1
  210.8 0.0 slice-done.2
  210.8 3.8 %fusion.4 = f32[256,1536]{1,0:T(8,128)} fusion(bf16[256,3072]{1,0:T(8,128)(2,1)S(1)} %bitcast.40, bf16[3072,1536]{1,0:T(8,128)(2,1)S(1)} %bitcast.48), kind=kOutput, calls=%fused_computation.15 | convolution fusion | flops 2415919104 | bytes 12582912 | tf_op jit(solution)/shard_map/dot_general | solution.py:344
  214.6 0.1 fusion.3
  214.7 1.5 multiply_exponential_fusion
  216.3 3.0 %convolution_convert_fusion.2 = bf16[6,128,256]{2,1,0:T(8,128)(2,1)} fusion(bf16[6,256,128]{2,1,0:T(8,128)(2,1)S(1)} %bitcast.45, f32[6,256,256]{1,2,0:T(8,128)} %multiply_exponential_fusion), kind=kOutput, calls=%fused_computation.6 | convolution fusion | flops 101648128 | bytes 2359296 | tf_op jit(solution)/shard_map/hbqk,hbke->bqhe/dot_general | solution.py:342
  219.3 0.0 copy-done
  219.3 2.3 fusion
  221.7 25.6 %total.1 = bf16[2,4,32,1536]{3,2,1,0:T(8,128)(2,1)S(1)} custom-call(bf16[2,4,32,1536]{3,2,1,0:T(8,128)(2,1)S(1)} %bitcast.33, bf16[2,4,32,1536]{3,2,1,0:T(8,128)(2,1)S(1)} %bitcast.38), custom_call_target="tpu_custom_call" | custom-call | tf_op jit(solution)/shard_map/total/pallas_call | solution.py:296
  247.2 0.9 copy.20
  (5 shorter events, 0.0 us)
Async XLA Ops:
  0.0 219.3 %copy-start = (bf16[768,1536]{1,0:T(8,128)(2,1)S(1)}, bf16[768,1536]{1,0:T(8,128)(2,1)}, u32[]{:S(2)}) copy-start(bf16[768,1536]{1,0:T(8,128)(2,1)} %param.22) | copy-start | bytes 7077892
  5.3 4.6 %copy-start.1 = (bf16[96,256,256]{2,1,0:T(8,128)(2,1)S(1)}, bf16[96,256,256]{2,1,0:T(8,128)(2,1)}, u32[]{:S(2)}) copy-start(bf16[96,256,256]{2,1,0:T(8,128)(2,1)} %pix_ref.1) | copy-start | bytes 37748740
  9.9 131.7 %copy-start.4 = (bf16[1536,3,768]{2,0,1:T(8,128)(2,1)S(1)}, bf16[1536,3,768]{2,0,1:T(8,128)(2,1)}, u32[]{:S(2)}) copy-start(bf16[1536,3,768]{2,0,1:T(8,128)(2,1)} %param.19) | copy-start | bytes 21233668
  141.6 3.7 %copy-start.3 = (bf16[1536,3072]{1,0:T(8,128)(2,1)S(1)}, bf16[1536,3072]{1,0:T(8,128)(2,1)}, u32[]{:S(2)}) copy-start(bf16[1536,3072]{1,0:T(8,128)(2,1)} %param.20) | copy-start | bytes 28311556
  141.6 69.2 %slice-start = ((s8[9437184]{0:T(1024)(128)(4,1)}), s8[4194304]{0:T(1024)(128)(4,1)S(1)}, s32[]{:S(2)}) async-start(s8[9437184]{0:T(1024)(128)(4,1)} %bitcast.47), calls=%async_computation | async-start | bytes 8388608
  141.6 69.2 %slice-start.1 = ((s8[9437184]{0:T(1024)(128)(4,1)}), s8[4194304]{0:T(1024)(128)(4,1)S(1)}, s32[]{:S(2)}) async-start(s8[9437184]{0:T(1024)(128)(4,1)} %bitcast.47), calls=%async_computation.1 | async-start | bytes 8388608
  145.2 2.6 %copy-start.2 = (f32[3072]{0:T(1024)S(1)}, f32[3072]{0:T(1024)}, u32[]{:S(2)}) copy-start(f32[3072]{0:T(1024)} %param.21) | copy-start | bytes 36868
  145.2 65.5 %slice-start.2 = ((s8[9437184]{0:T(1024)(128)(4,1)}), s8[1048576]{0:T(1024)(128)(4,1)S(1)}, s32[]{:S(2)}) async-start(s8[9437184]{0:T(1024)(128)(4,1)} %bitcast.47), calls=%async_computation.2 | async-start | bytes 2097152
where the time goes:
time: 250 us; the launch traced here: 248 us
  Pallas kernels  220 us (88%)
  matrix products  15.3 us (6%)
  local copies, waits for them, and re-layouts  10.6 us (4%)
    pallas_call x1, Pallas kernels, pool(): pl.pallas_call(functools.partial(pool_kernel, size), grid_spec=spec, out_...  99.9 us
    pallas_call x1, Pallas kernels, finish(): pl.pallas_call(functools.partial(finish_kernel, chans, hids, heads), out_...  62.9 us
    pallas_call x1, Pallas kernels, layer_rows(): pl.pallas_call(functools.partial(layer_kernel, chans, hids), out_shape=(s...  31.7 us
    pallas_call x1, Pallas kernels, total(): pl.pallas_call(functools.partial(total_kernel, hids), out_shape=jax.Shape...  25.6 us
    unnamed x17, local copies, waits for them, and re-layouts  7.13 us

commit v1 on v0

--- a/solution.py
+++ b/solution.py
@@ -15,95 +15,130 @@
 epsilon = 1e-06
 
 
-def pool_kernel(size, order_ref, pix_ref, pw_ref, emb_ref, query_ref, shift_ref, mix_ref, out_ref, feat, sq, numer, denom, acc, pick, quer):
-    g = pl.program_id(0); j = pl.program_id(1)
-    tok, width = acc.shape
-    heads = width // HS
-    head = lax.broadcasted_iota(jnp.int32, (HS, width), 0)
-    head_of = lax.broadcasted_iota(jnp.int32, (HS, width), 1) // HS
-
-    @pl.when((g == 0) & (j == 0))
+ACROSS = (((1,), (1,)), ((), ()))
+LOG2E = math.log2(math.e)
+SLOT = 16
+ROWS = 256
+CPS = 4
+
+
+def pool_setup(groups, size, query, mix, emb, quer, pick, shift, mixs, embs, fan):
+    width = quer.shape[1]
+    own = lax.broadcasted_iota(jnp.int32, (SLOT, width), 0) == lax.broadcasted_iota(jnp.int32, (SLOT, width), 1) // HS
+    q = query[...].astype(jnp.float32)
+    m = mix[...].astype(jnp.float32) * math.sqrt(0.5)
+    pick[...] = jnp.where(own, 1.0, 0.0).astype(jnp.bfloat16)
+    for g in range(groups):
+        row = jnp.where(own, q[g:g+1, :], 0.0)
+        rs = slice(g*SLOT, (g+1)*SLOT)
+        quer[rs, :] = row.astype(jnp.bfloat16)
+        n = jnp.sqrt(jnp.sum(row * row, axis=1, keepdims=True)) * LOG2E
+        shift[rs, :] = jnp.broadcast_to(n, (SLOT, HS))
+        mixs[g] = m[g:g+1]
+    for c in range(0, emb.shape[0], 8):
+        e = emb[c:c+8, :].astype(jnp.float32) * math.sqrt(0.5)
+        for k in range(8):
+            embs[c+k] = e[k:k+1]
+    kind = lax.rem(lax.broadcasted_iota(jnp.int32, (HS, width), 0), HS // 2)
+    head = lax.broadcasted_iota(jnp.int32, (HS, width), 1) // HS
+    for j in range(size):
+        fan[j] = jnp.where(kind == j * 8 + head, 1.0, 0.0).astype(jnp.bfloat16)
+
+def features(tok, px_of, pw_of, bias, put):
+    width = bias.shape[1]
+    step = min(256, width)
+    R = min(ROWS, tok)
+    for n in range(width // step):
+        cs = slice(n*step, (n+1)*step)
+        for r in range(0, tok, R):
+            e = jnp.dot(px_of(r, R), pw_of(cs), preferred_element_type=jnp.float32)
+            u = e * math.sqrt(0.5) + bias[:, cs]
+            g = (u * (1.0 + lax.erf(u))).astype(jnp.bfloat16)
+            put(r, R, cs, g, g * g)
+
+def weigh(tok, g, s, local, quer, pick, shift):
+    rs = pl.ds(pl.multiple_of(local * SLOT, SLOT), SLOT)
+    dots = lax.dot_general(quer[rs, :], g[...], ACROSS, preferred_element_type=jnp.float32)
+    total = lax.dot_general(pick[...], s[...], ACROSS, preferred_element_type=jnp.float32)
+    sh = jnp.concatenate([shift[rs, :]] * (tok // HS), axis=1)
+    score = dots * lax.rsqrt(total * (1.0 / HS) + 2 * epsilon) * (LOG2E / math.sqrt(HS))
+    return jnp.exp2(score - sh)[0:8, :]
+
+def merge(groups, size, tok, order, feat, wts, mixs, fan, acc):
+    width = feat.shape[2]
+    step = min(256, width)
+    def group(g, _):
+        cs = [order[g*size + j] for j in range(size)]
+        for b in range(0, tok, HS):
+            bs = slice(b, b + HS)
+            ws = [wts[c, :, bs] for c in cs]
+            den = ws[0]
+            for w in ws[1:]:
+                den = den + w
+            inv = 1.0 / den
+            w = jnp.concatenate([w * inv for w in ws], axis=0)
+            hi = w.astype(jnp.bfloat16).astype(jnp.float32)
+            both = jnp.transpose(jnp.concatenate([hi, w - hi], axis=0))
+            lhs = both.astype(jnp.bfloat16)
+            for n in range(width // step):
+                ns = slice(n*step, (n+1)*step)
+                p = None
+                for j in range(size):
+                    t = jnp.dot(lhs, fan[j, :, ns], preferred_element_type=jnp.float32) * feat[cs[j], bs, ns].astype(jnp.float32)
+                    p = t if p is None else p + t
+                acc[bs, ns] += p * mixs[g, :, ns]
+        return 0
+    lax.fori_loop(0, groups, group, 0)
+
+def pool_kernel(groups, size, order, assign, pix, pw, emb, query, mix, out, feat, wts, acc, quer, pick, shift, mixs, embs, fan, g0, g1, s0, s1):
+    t = pl.program_id(0); c = pl.program_id(1)
+    tok = out.shape[0]
+    gb, sb = (g0, g1), (s0, s1)
+    @pl.when((t == 0) & (c == 0))
+    def _():
+        pool_setup(groups, size, query, mix, emb, quer, pick, shift, mixs, embs, fan)
+    @pl.when(c == 0)
     def _():
         acc[...] = jnp.zeros_like(acc)
-        pick[...] = jnp.where(head_of == head, 1.0, 0.0).astype(jnp.bfloat16)
-
-    @pl.when(j == 0)
+    def back(k):
+        cc = c * CPS + k
+        wts[cc] = weigh(tok, gb[k % 2], sb[k % 2], lax.rem(assign[cc], groups), quer, pick, shift)
+    for k in range(CPS):
+        cc = c * CPS + k
+        def put(r, R, cs, g, s):
+            feat[cc, r:r+R, cs] = g
+            gb[k % 2][r:r+R, cs] = g
+            sb[k % 2][r:r+R, cs] = s
+        features(tok, lambda r, R: pix[k, r:r+R, :], lambda cs: pw[k, :, cs], embs[cc], put)
+        if k: back(k - 1)
+    back(CPS - 1)
+    @pl.when(c == pl.num_programs(1)-1)
     def _():
-        quer[...] = jnp.where(head_of == head, query_ref[0], 0.0).astype(jnp.bfloat16)
-
-    across = (((1,), (1,)), ((), ()))
-    step = min(256, width)
-    for n in range(width // step):
-        cs = slice(n * step, (n + 1) * step)
-        for r in range(0, tok, 64):
-            e = jnp.dot(pix_ref[0, r:r+64], pw_ref[0, :, cs], preferred_element_type=jnp.float32)
-            e = e + emb_ref[0, :, cs]
-            f = (0.5 * e) * (1.0 + lax.erf(e * math.sqrt(0.5)))
-            feat[r:r+64, cs] = f.astype(jnp.bfloat16)
-            sq[r:r+64, cs] = (f * f).astype(jnp.bfloat16)
-    dots = lax.dot_general(feat[...], quer[...], across, preferred_element_type=jnp.float32)
-    total = lax.dot_general(sq[...], pick[...], across, preferred_element_type=jnp.float32)
-    score = dots * lax.rsqrt(total * (1.0 / HS) + epsilon) * (1.0 / math.sqrt(HS))
-    weight = jnp.exp(score - shift_ref[0])
-    @pl.when(j == 0)
-    def _():
-        denom[...] = weight
-        for h in range(heads):
-            hs = slice(h * HS, (h + 1) * HS)
-            numer[:, hs] = weight[:, h:h+1] * feat[:, hs].astype(jnp.float32)
-    @pl.when(j > 0)
-    def _():
-        denom[...] += weight
-        for h in range(heads):
-            hs = slice(h * HS, (h + 1) * HS)
-            numer[:, hs] += weight[:, h:h+1] * feat[:, hs].astype(jnp.float32)
-    @pl.when(j == size - 1)
-    def _():
-        inv = 1.0 / denom[...]
-        for h in range(heads):
-            hs = slice(h * HS, (h + 1) * HS)
-            acc[:, hs] += numer[:, hs] * inv[:, h:h+1] * mix_ref[0, :, hs]
-    @pl.when((g == pl.num_programs(0) - 1) & (j == size - 1))
-    def _():
-        out_ref[...] = acc[...].astype(jnp.bfloat16)
-
-def pool(pixels, patch_weight, channel_embed, pool_query, group_mix, assign):
+        merge(groups, size, tok, order, feat, wts, mixs, fan, acc)
+        out[...] = acc[...].astype(jnp.bfloat16)
+
+def pool(T, pixels, patch_weight, channel_embed, pool_query, group_mix, assign):
     chans, tok, p2 = pixels.shape
     width = patch_weight.shape[2]
     groups = pool_query.shape[0]
     size = chans // groups
-    heads = width // HS
     idx = jnp.arange(chans, dtype=jnp.int32)
     key = assign * chans + idx
     rank = jnp.sum((key[None, :] < key[:, None]).astype(jnp.int32), axis=1)
     order = jnp.sum(jnp.where(rank[None, :] == idx[:, None], idx[None, :], 0), axis=1).astype(jnp.int32)
-    q = pool_query.astype(jnp.float32)
-    sh = jnp.sqrt(jnp.sum((q * q).reshape(groups, heads, HS), axis=-1))
-    sh = jnp.pad(sh, ((0, 0), (0, HS - heads))).reshape(groups, 1, HS)
-    spec = pltpu.PrefetchScalarGridSpec(
-        num_scalar_prefetch=1, grid=(groups, size),
-        in_specs=[
-            pl.BlockSpec((1, tok, p2), lambda g, j, o: (o[g * size + j], 0, 0)),
-            pl.BlockSpec((1, p2, width), lambda g, j, o: (o[g * size + j], 0, 0)),
-            pl.BlockSpec((1, 1, width), lambda g, j, o: (o[g * size + j], 0, 0)),
-            pl.BlockSpec((1, 1, width), lambda g, j, o: (g, 0, 0)),
-            pl.BlockSpec((1, 1, HS), lambda g, j, o: (g, 0, 0)),
-            pl.BlockSpec((1, 1, width), lambda g, j, o: (g, 0, 0)),
-        ],
-        out_specs=pl.BlockSpec((tok, width), lambda g, j, o: (0, 0)),
-        scratch_shapes=[
-            pltpu.VMEM((tok, width), jnp.bfloat16), pltpu.VMEM((tok, width), jnp.bfloat16),
-            pltpu.VMEM((tok, width), jnp.float32), pltpu.VMEM((tok, HS), jnp.float32),
-            pltpu.VMEM((tok, width), jnp.float32), pltpu.VMEM((HS, width), jnp.bfloat16), pltpu.VMEM((HS, width), jnp.bfloat16)])
-    return pl.pallas_call(
-        functools.partial(pool_kernel, size), grid_spec=spec,
-        out_shape=jax.ShapeDtypeStruct((tok, width), jnp.bfloat16),
-        compiler_params=pltpu.CompilerParams(dimension_semantics=("arbitrary", "arbitrary"), vmem_limit_bytes=40 << 20),
-        name="pool",
-    )(order, pixels, patch_weight, channel_embed.astype(jnp.float32).reshape(chans, 1, width), q.reshape(groups, 1, width), sh,
-      group_mix.astype(jnp.float32).reshape(groups, 1, width))
-
-
+    full = lambda s: pl.BlockSpec(s, lambda t, c, *_: (0,)*len(s))
+    vm = pltpu.VMEM
+    spec = pltpu.PrefetchScalarGridSpec(num_scalar_prefetch=2, grid=(tok//T, chans//CPS),
+        in_specs=[pl.BlockSpec((CPS,T,p2), lambda t,c,*_:(c,t,0)), pl.BlockSpec((CPS,p2,width), lambda t,c,*_:(c,0,0)),
+          full((chans,width)), full((groups,width)), full((groups,width))],
+        out_specs=pl.BlockSpec((T,width), lambda t,c,*_:(t,0)),
+        scratch_shapes=[vm((chans,T,width), jnp.bfloat16), vm((chans,8,T), jnp.float32),
+          vm((T,width), jnp.float32), vm((groups*SLOT,width), jnp.bfloat16), vm((SLOT,width), jnp.bfloat16),
+          vm((groups*SLOT,HS), jnp.float32), vm((groups,1,width), jnp.float32), vm((chans,1,width), jnp.float32),
+          vm((size,HS,width), jnp.bfloat16)] + [vm((T,width), jnp.bfloat16)]*4)
+    return pl.pallas_call(functools.partial(pool_kernel, groups, size), grid_spec=spec, out_shape=jax.ShapeDtypeStruct((tok,width), jnp.bfloat16),
+        compiler_params=pltpu.CompilerParams(dimension_semantics=("arbitrary","arbitrary"), vmem_limit_bytes=62<<20), name="pool")(
+        order, assign, pixels, patch_weight, channel_embed, pool_query, group_mix)
 def head_norm(values):
     return values * lax.rsqrt(jnp.mean(values * values, axis=-1, keepdims=True) + epsilon)
 
@@ -325,7 +360,7 @@
     tok_count = pixels.shape[1]
     width_hid = patch_weight.shape[2]
     heads_dev = width_hid // HS
-    partial_value = pool(pixels, patch_weight, channel_embed, pool_query, group_mix, assign)
+    partial_value = pool(pixels.shape[1], pixels, patch_weight, channel_embed, pool_query, group_mix, assign)
     normed_input, own_cols = layer_rows(partial_value, ln_gain, chans, hids)
     qkv_part = jnp.einsum("td,dke->kte", normed_input, w_qkv, preferred_element_type=jnp.float32)
     up_part = jnp.dot(normed_input, w_up, preferred_element_type=jnp.float32)

time: 250 us -> 197 us (0.79)
  Pallas kernels: 220 us -> 172 us
  local copies, waits for them, and re-layouts: 10.6 us -> 3.22 us
  matrix products: 15.3 us -> 18.6 us
    pallas_call x1, Pallas kernels: 99.9 us -> 52.2 us  [pool(): pl.pallas_call(functools.partial(pool_kernel, groups, size), grid_spec=sp...]
    unnamed x17 -> x15, local copies, waits for them, and re-layouts: 7.13 us -> 2.41 us
    dot_general x1, matrix products: 1.99 us -> 5.15 us  [on_device(): jnp.einsum('td,dke->kte', normed_input, w_qkv, preferred_element_type=jnp...]
    reshape x5 -> x0, local copies, waits for them, and re-layouts: 2.6 us -> none  [the longest x1 1.07 us: pool(): channel_embed.astype(jnp.float32).reshape(chans, 1, width)]
where the time goes in v1:
time: 197 us; the launch traced here: 196 us
  Pallas kernels  172 us (87%)
  matrix products  18.6 us (9%)
  local copies, waits for them, and re-layouts  3.22 us (2%)
    pallas_call x1, Pallas kernels, finish(): pl.pallas_call(functools.partial(finish_kernel, chans, hids, heads), out_...  62.9 us
    pallas_call x1, Pallas kernels, pool(): pl.pallas_call(functools.partial(pool_kernel, groups, size), grid_spec=sp...  52.2 us
    pallas_call x1, Pallas kernels, layer_rows(): pl.pallas_call(functools.partial(layer_kernel, chans, hids), out_shape=(s...  31.6 us
    pallas_call x1, Pallas kernels, total(): pl.pallas_call(functools.partial(total_kernel, hids), out_shape=jax.Shape...  25.6 us
    dot_general x1, matrix products, on_device(): jnp.einsum('td,dke->kte', normed_input, w_qkv, preferred_element_type=jnp...  5.15 us

profile of v1, /device:TPU:25, one launch (start us, length us, event | category | flops | bytes accessed | tf_op | source)
XLA Modules:
  0.0 195.7 jit_solution(9143366377095203891)
XLA Ops:
  0.0 0.7 iota_add_fusion
  0.7 0.2 convert_reduce_fusion
  0.8 0.6 select_reduce_fusion.order
  1.5 0.7 reshape.66.gain
  2.2 52.2 %pool.1 = bf16[256,768]{1,0:T(8,128)(2,1)} custom-call(s32[96]{0:T(128)} %select_reduce_fusion.order, s32[96]{0:T(128)} %assign.1, bf16[96,256,256]{2,1,0:T(8,128)(2,1)} %pix.1, bf16[96,256,768]{2,1,0:T(8,128)(2,1)} %pw.1, bf16[96,768]{1,0:T(8,128)(2,1)} %emb.1, bf16[12,768]{1,0:T(8,128)(2,1)} %query.1, bf16[12,768]{1,0:T(8,128)(2,1)} %mix.1), custom_call_target="tpu_custom_call" | custom-call | tf_op jit(solution)/shard_map/pool/pallas_call | solution.py:139
  54.4 0.0 copy-start
  54.4 1.0 copy-done
  55.4 31.6 %layer_rows.1 = (bf16[4,64,1536]{2,1,0:T(8,128)(2,1)S(1)}, bf16[4,64,1536]{2,1,0:T(8,128)(2,1)S(1)}) custom-call(bf16[4,64,768]{2,1,0:T(8,128)(2,1)S(1)} %bitcast.35, f32[1,1536]{1,0:T(1,128)S(1)} %reshape.66.gain), custom_call_target="tpu_custom_call" | custom-call | tf_op jit(solution)/shard_map/layer_rows/pallas_call | solution.py:240
  87.1 0.0 copy-start.3
  87.1 0.0 slice-start
  87.1 0.0 slice-start.1
  87.1 5.2 %convolution_convert_fusion.1 = bf16[256,3,768]{2,0,1:T(8,128)(2,1)S(1)} fusion(bf16[256,1536,1]{1,0,2:T(8,128)(2,1)S(1)} %bitcast.41, bf16[1536,3,768]{2,0,1:T(8,128)(2,1)} %param.19), kind=kOutput, calls=%fused_computation.5 | convolution fusion | flops 1812529152 | bytes 9043968 | tf_op jit(solution)/shard_map/td,dke->kte/dot_general | solution.py:365
  92.3 0.5 copy-done.3
  92.8 0.0 copy-start.1
  92.8 0.0 slice-start.2
  92.8 2.6 %convolution_convert_fusion = bf16[256,3072]{1,0:T(8,128)(2,1)S(1)} fusion(bf16[256,1536]{1,0:T(8,128)(2,1)S(1)} %bitcast.42, bf16[1536,3072]{1,0:T(8,128)(2,1)S(1)} %copy-done.3), kind=kOutput, calls=%fused_computation | convolution fusion | flops 2416705536 | bytes 11796480 | tf_op jit(solution)/shard_map/dot_general | solution.py:366
  95.4 0.0 copy-done.1
  95.4 62.9 %finish.1 = (bf16[18,4,64,128]{3,2,1,0:T(8,128)(2,1)S(1)}, bf16[4,64,3072]{2,1,0:T(8,128)(2,1)S(1)}) custom-call(bf16[3,4,64,768]{3,2,1,0:T(8,128)(2,1)S(1)} %bitcast.37, bf16[4,64,3072]{2,1,0:T(8,128)(2,1)S(1)} %bitcast.36, f32[1,3072]{1,0:T(1,128)S(1)} %bitcast.39), custom_call_target="tpu_custom_call" | custom-call | tf_op jit(solution)/shard_map/finish/pallas_call | solution.py:291
  158.3 0.0 slice-done
  158.3 0.0 slice-done.1
  158.3 0.0 slice-done.2
  158.3 3.8 %fusion.4 = f32[256,1536]{1,0:T(8,128)} fusion(bf16[256,3072]{1,0:T(8,128)(2,1)S(1)} %bitcast.40, bf16[3072,1536]{1,0:T(8,128)(2,1)S(1)} %bitcast.48), kind=kOutput, calls=%fused_computation.14 | convolution fusion | flops 2415919104 | bytes 12582912 | tf_op jit(solution)/shard_map/dot_general | solution.py:379
  162.1 0.1 fusion.3
  162.2 1.5 multiply_exponential_fusion
  163.7 0.0 copy-start.2
  163.7 3.2 %convolution_convert_fusion.2 = bf16[6,128,256]{2,1,0:T(8,128)(2,1)} fusion(bf16[6,256,128]{2,1,0:T(8,128)(2,1)S(1)} %bitcast.45, f32[6,256,256]{1,2,0:T(8,128)} %multiply_exponential_fusion), kind=kOutput, calls=%fused_computation.6 | convolution fusion | flops 101648128 | bytes 2359296 | tf_op jit(solution)/shard_map/hbqk,hbke->bqhe/dot_general | solution.py:377
  166.9 0.0 copy-done.2
  166.9 2.3 %fusion = bf16[256,1536]{1,0:T(8,128)(2,1)S(1)} fusion(f32[256,1536]{1,0:T(8,128)} %fusion.4, bf16[256,768]{0,1:T(8,128)(2,1)} %bitcast.46, bf16[768,1536]{1,0:T(8,128)(2,1)S(1)} %copy-done.2), kind=kOutput, calls=%fused_computation.2 | convolution fusion | flops 604766208 | bytes 5111808 | tf_op jit(solution)/shard_map/dot_general | solution.py:379
  169.2 25.6 %total.1 = bf16[2,4,32,1536]{3,2,1,0:T(8,128)(2,1)S(1)} custom-call(bf16[2,4,32,1536]{3,2,1,0:T(8,128)(2,1)S(1)} %bitcast.33, bf16[2,4,32,1536]{3,2,1,0:T(8,128)(2,1)S(1)} %bitcast.38), custom_call_target="tpu_custom_call" | custom-call | tf_op jit(solution)/shard_map/total/pallas_call | solution.py:331
  194.8 0.9 copy.20
  (1 shorter events, 0.0 us)
Async XLA Ops:
  54.4 1.0 copy-start
  87.1 5.7 %copy-start.3 = (bf16[1536,3072]{1,0:T(8,128)(2,1)S(1)}, bf16[1536,3072]{1,0:T(8,128)(2,1)}, u32[]{:S(2)}) copy-start(bf16[1536,3072]{1,0:T(8,128)(2,1)} %param.20) | copy-start | bytes 28311556
  87.1 71.2 %slice-start = ((s8[9437184]{0:T(1024)(128)(4,1)}), s8[4194304]{0:T(1024)(128)(4,1)S(1)}, s32[]{:S(2)}) async-start(s8[9437184]{0:T(1024)(128)(4,1)} %bitcast.47), calls=%async_computation | async-start | bytes 8388608
  87.1 71.2 %slice-start.1 = ((s8[9437184]{0:T(1024)(128)(4,1)}), s8[4194304]{0:T(1024)(128)(4,1)S(1)}, s32[]{:S(2)}) async-start(s8[9437184]{0:T(1024)(128)(4,1)} %bitcast.47), calls=%async_computation.1 | async-start | bytes 8388608
  92.8 2.6 %copy-start.1 = (f32[3072]{0:T(1024)S(1)}, f32[3072]{0:T(1024)}, u32[]{:S(2)}) copy-start(f32[3072]{0:T(1024)} %param.21) | copy-start | bytes 36868
  92.8 65.5 %slice-start.2 = ((s8[9437184]{0:T(1024)(128)(4,1)}), s8[1048576]{0:T(1024)(128)(4,1)S(1)}, s32[]{:S(2)}) async-start(s8[9437184]{0:T(1024)(128)(4,1)} %bitcast.47), calls=%async_computation.2 | async-start | bytes 2097152
  163.7 3.2 %copy-start.2 = (bf16[768,1536]{1,0:T(8,128)(2,1)S(1)}, bf16[768,1536]{1,0:T(8,128)(2,1)}, u32[]{:S(2)}) copy-start(bf16[768,1536]{1,0:T(8,128)(2,1)} %param.22) | copy-start | bytes 7077892

commit v2 on v1

--- a/solution.py
+++ b/solution.py
@@ -341,6 +341,369 @@
     return out.reshape(tok, wide)
 
 
+def column_steps(width, most=384):
+    step = max(s for s in range(HS, most + 1, HS) if width % s == 0)
+    return [slice(n, n + step) for n in range(0, width, step)]
+
+
+class Tail:
+    def __init__(self, chans, hids, refs):
+        self.__dict__.update(refs)
+        self.chans, self.hids = chans, hids
+        self.a, self.b, self.chips, self.chip, self.core, self.rows, self.far, self.mate = places(chans, hids)
+        self.y, self.x = self.a // 2, self.a % 2
+        self.across_x, self.across_y = {"chan": self.y * 2 + 1 - self.x}, {"chan": (1 - self.y) * 2 + self.x}
+        self.used, self.open = 0, []
+
+    def put(self, src, dst, peer):
+        slot = self.used
+        self.used += 1
+        copy = pltpu.make_async_remote_copy(
+            src_ref=src, dst_ref=dst, send_sem=self.sems.at[0, slot], recv_sem=self.sems.at[1, slot],
+            device_id=peer, device_id_type=MESH)
+        copy.start()
+        self.open.append(copy)
+        return copy
+
+    def drain(self):
+        for copy in self.open:
+            copy.wait_send()
+
+    def scatter(self, t):
+        a, chans = self.a, self.chans
+        self.s_copies = getattr(self, "s_copies", {})
+        self.s_copies[t] = [
+            self.put(self.part.at[t, lax.rem(a + k, chans)], self.parts.at[t, k - 1], self.rows[k - 1]) for k in range(1, chans)]
+
+    def collect(self, t):
+        total = self.part[t, self.a].astype(jnp.float32)
+        for k, copy in enumerate(self.s_copies[t]):
+            copy.wait_recv()
+            total = total + self.parts[t, k].astype(jnp.float32)
+        b = self.b
+        self.gath[t, b] = total.astype(jnp.bfloat16)
+        mine = self.gath.at[t, b]
+        self.g_far = getattr(self, "g_far", {})
+        self.g_near = getattr(self, "g_near", {})
+        self.g_far[t] = [self.put(mine, mine, peer) for peer in self.far]
+        self.g_near[t] = [self.put(mine, mine, self.mate)]
+
+    def relay(self, t):
+        for k in range(1, self.chips):
+            self.g_far[t][k - 1].wait_recv()
+            piece = self.gath.at[t, lax.rem(self.chip + self.chips - k, self.chips) * 2 + self.core]
+            self.g_near[t].append(self.put(piece, piece, self.mate))
+
+    def exchange(self, t):
+        for copy in self.g_near[t]:
+            copy.wait_recv()
+        size, width = self.gath.shape[2:]
+        first = jnp.zeros((size, 1), jnp.float32)
+        second = jnp.zeros((size, 1), jnp.float32)
+        for i in range(self.hids):
+            x = self.gath[t, i].astype(jnp.float32)
+            first = first + jnp.sum(x, axis=1, keepdims=True)
+            second = second + jnp.sum(x * x, axis=1, keepdims=True)
+        mean = first / (width * self.hids)
+        scale = lax.rsqrt(second / (width * self.hids) - mean * mean + epsilon)
+        self.stat[t] = jnp.where(lax.broadcasted_iota(jnp.int32, (size, HS), 1) == 0, mean, scale)
+        self.c_stat = getattr(self, "c_stat", {})
+        self.c_piece = getattr(self, "c_piece", {})
+        a, chans = self.a, self.chans
+        self.c_stat[t] = [self.put(self.stat.at[t], self.stats.at[t, a], peer) for peer in self.rows]
+        self.c_piece[t] = [
+            self.put(self.gath.at[t, lax.rem(a + k, chans) * 2 + self.core], self.whole.at[t, a, self.core], self.rows[k - 1])
+            for k in range(1, chans)]
+
+    def share(self, t):
+        self.c_near = getattr(self, "c_near", {})
+        self.c_near[t] = []
+        for k in range(1, self.chans):
+            self.c_piece[t][k - 1].wait_recv()
+            piece = self.whole.at[t, lax.rem(self.a + self.chans - k, self.chans), self.core]
+            self.c_near[t].append(self.put(piece, piece, self.mate))
+
+    def norm(self, t):
+        size, width = self.gath.shape[2:]
+
+        def emit(i, x_of, st):
+            for r in range(2):
+                cs = slice(r * width, (r + 1) * width)
+                x = x_of(r)
+                self.own[t, i, :, cs] = x
+                self.normed[t, i, :, cs] = (
+                    (x.astype(jnp.float32) - st[:, 0:1]) * st[:, 1:2] * self.gain[:, cs]).astype(jnp.bfloat16)
+
+        emit(self.a, lambda r: self.gath[t, self.a * 2 + r], self.stat[t])
+        for copy in self.c_stat[t] + self.c_near[t]:
+            copy.wait_recv()
+        for k in range(1, self.chans):
+            i = lax.rem(self.a + k, self.chans)
+            emit(i, lambda r: self.whole[t, i, r], self.stats[t, i])
+
+    def multiply(self, t, kind):
+        buf, weights = self.units[kind][0], self.units[kind][4]
+        size = buf.shape[3]
+        wide = buf.shape[4]
+        step = min(256, self.w_qkv.shape[2])
+        x = self.normed[t].reshape(4 * size, self.normed.shape[3])
+        per = weights.shape[-1]
+
+        for k in range(wide // per):
+            def tile(n, _):
+                off = pl.multiple_of(n * step, step)
+                w = weights[k, :, pl.ds(off, step)] if kind == "qkv" else weights[:, pl.ds(off, step)]
+                e = jnp.dot(x, w, preferred_element_type=jnp.float32).astype(jnp.bfloat16)
+                buf[t, :, :, :, pl.ds(pl.multiple_of(k * per + off, step), step)] = e.reshape(2, 2, size, step)
+                return 0
+            lax.fori_loop(0, per // step, tile, 0)
+
+    def halves(self, kind):
+        wide = self.units[kind][0].shape[4]
+        return slice(0, wide // 2), slice(wide // 2, wide)
+
+    def reduce1(self, t, kind):
+        buf, got1 = self.units[kind][:2]
+        left, right = self.halves(kind)
+        self.d1 = getattr(self, "d1", {})
+        self.d1[t, kind] = (
+            self.put(buf.at[t, :, 1 - self.x, :, left], got1.at[t, 0], self.across_x),
+            self.put(buf.at[t, 1 - self.y, :, :, right], got1.at[t, 1], self.across_y))
+
+    def reduce2(self, t, kind):
+        buf, got1, mid, got2 = self.units[kind][:4]
+        left, right = self.halves(kind)
+        self.d2 = getattr(self, "d2", {})
+        for copy in self.d1[t, kind]:
+            copy.wait_recv()
+        for side in range(2):
+            base = (left, right)[side].start
+            for cs in column_steps(got1.shape[4]):
+                here = slice(base + cs.start, base + cs.stop)
+                mine = buf[t, 1 - self.y, self.x, :, here] if side == 0 else buf[t, self.y, 1 - self.x, :, here]
+                got = got1[t, 0, 1 - self.y, :, cs] if side == 0 else got1[t, 1, 1 - self.x, :, cs]
+                mid[t, side, :, cs] = (mine.astype(jnp.float32) + got.astype(jnp.float32)).astype(jnp.bfloat16)
+            self.d2[t, kind, side] = self.put(mid.at[t, side], got2.at[t, side], (self.across_y, self.across_x)[side])
+
+    def act(self, t, kind):
+        buf, got1, _, got2, _, full = self.units[kind]
+        left, right = self.halves(kind)
+        self.e1 = getattr(self, "e1", {})
+        rotated = 2 * self.w_qkv.shape[2]
+        for side in range(2):
+            self.d2[t, kind, side].wait_recv()
+            base = (left, right)[side].start
+            for c in range(0, got1.shape[4], HS):
+                cs = slice(c, c + HS)
+                here = slice(base + c, base + c + HS)
+                v = buf[t, self.y, self.x, :, here].astype(jnp.float32) + got2[t, side, :, cs].astype(jnp.float32)
+                v = v + (got1[t, 0, self.y, :, cs] if side == 0 else got1[t, 1, self.x, :, cs]).astype(jnp.float32)
+                if kind == "up":
+                    v = v + self.bias[:, here]
+                    v = (0.5 * v) * (1.0 + lax.erf(v * math.sqrt(0.5)))
+                elif base + c < rotated:
+                    v = v * lax.rsqrt(jnp.mean(v * v, axis=-1, keepdims=True) + epsilon)
+                full[t, self.y, self.x, :, here] = v.astype(jnp.bfloat16)
+            mine = full.at[t, self.y, self.x, :, (left, right)[side]]
+            self.e1[t, kind, side] = self.put(mine, mine, (self.across_y, self.across_x)[side])
+
+    def gather2(self, t, kind):
+        full = self.units[kind][5]
+        left, right = self.halves(kind)
+        self.e2 = getattr(self, "e2", {})
+        for side in range(2):
+            self.e1[t, kind, side].wait_recv()
+            mine = full.at[t, :, self.x, :, left] if side == 0 else full.at[t, self.y, :, :, right]
+            self.e2[t, kind, side] = self.put(mine, mine, (self.across_x, self.across_y)[side])
+
+    def whole_unit(self, t, kind):
+        for side in range(2):
+            self.e2[t, kind, side].wait_recv()
+
+    def attend(self, chunks):
+        full = self.units["qkv"][5]
+        size = full.shape[3]
+        wide = self.w_qkv.shape[2]
+        tok = chunks * 4 * size
+
+        def head(h, _):
+            def take(kind):
+                cs = pl.ds(pl.multiple_of(kind * wide + h * HS, HS), HS)
+                return full[:, :, :, :, cs].reshape(tok, HS)
+            q, k, v = take(0), take(1), take(2)
+            for r in range(0, tok, PATCHES):
+                rs = slice(r, r + PATCHES)
+                scores = lax.dot_general(q[rs], k[rs], ACROSS, preferred_element_type=jnp.float32) * (2.0 / math.sqrt(HS))
+                expo = jnp.exp(scores)
+                probs = (expo * (1.0 / jnp.sum(expo, axis=-1, keepdims=True))).astype(jnp.bfloat16)
+                got = jnp.dot(probs, v[rs], preferred_element_type=jnp.float32).astype(jnp.bfloat16)
+                self.attended[rs, pl.ds(pl.multiple_of(h * HS, HS), HS)] = got
+            return 0
+
+        lax.fori_loop(0, wide // HS, head, 0)
+
+    def down(self, t):
+        full = self.units["up"][5]
+        size = full.shape[3]
+        rows = 4 * size
+        wide = self.w_out.shape[1]
+        step = min(256, wide)
+        hidden = full[t].reshape(rows, full.shape[4])
+        att = self.attended[t * rows:(t + 1) * rows]
+
+        def tile(n, _):
+            cs = pl.ds(pl.multiple_of(n * step, step), step)
+            e = jnp.dot(hidden, self.w_down[:, cs], preferred_element_type=jnp.float32)
+            e = e + jnp.dot(att, self.w_out[:, cs], preferred_element_type=jnp.float32)
+            self.term[t, :, :, :, cs] = e.astype(jnp.bfloat16).reshape(2, self.chips, rows // self.hids, step)
+            return 0
+
+        lax.fori_loop(0, wide // step, tile, 0)
+        self.f1 = getattr(self, "f1", {})
+        self.f1[t] = self.put(self.term.at[t, 1 - self.core], self.pair.at[t], self.mate)
+
+    def total1(self, t):
+        self.f1[t].wait_recv()
+        self.f2 = getattr(self, "f2", {})
+        chips, chip = self.chips, self.chip
+        for i in range(chips):
+            self.half[t, i] = (
+                self.term[t, self.core, i].astype(jnp.float32) + self.pair[t, i].astype(jnp.float32)).astype(jnp.bfloat16)
+        self.f2[t] = [
+            self.put(self.half.at[t, lax.rem(chip + k, chips)], self.pieces.at[t, k - 1], self.far[k - 1]) for k in range(1, chips)]
+
+    def total2(self, t):
+        value = self.half[t, self.chip].astype(jnp.float32)
+        for k, copy in enumerate(self.f2[t]):
+            copy.wait_recv()
+            value = value + self.pieces[t, k].astype(jnp.float32)
+        core, chip, chips = self.core, self.chip, self.chips
+        own = self.own_rows(t)
+        self.out[t, core, chip] = (value + own).astype(jnp.bfloat16)
+        mine = self.out.at[t, core, chip]
+        self.f3 = getattr(self, "f3", {})
+        self.f4 = getattr(self, "f4", {})
+        self.f3[t] = [self.put(mine, mine, peer) for peer in self.far]
+        self.f4[t] = [self.put(mine, mine, self.mate)]
+
+    def own_rows(self, t):
+        rows = self.out.shape[3]
+        place = (self.core * self.chips + self.chip) * rows
+        size = self.own.shape[2]
+        return self.own[t, place // size, pl.ds(pl.multiple_of(lax.rem(place, size), rows), rows), :].astype(jnp.float32)
+
+    def total3(self, t):
+        for k in range(1, self.chips):
+            self.f3[t][k - 1].wait_recv()
+            piece = self.out.at[t, self.core, lax.rem(self.chip + self.chips - k, self.chips)]
+            self.f4[t].append(self.put(piece, piece, self.mate))
+
+    def total4(self, t):
+        for copy in self.f4[t]:
+            copy.wait_recv()
+
+
+def tail_kernel(chans, hids, chunks, *refs):
+    names = ["part", "gain", "bias", "wq_hbm", "wu_hbm", "wo_hbm", "wd_hbm", "out", "parts", "gath", "stat", "stats", "whole",
+             "own", "normed", "q0", "q1", "q2", "q3", "q4", "u0", "u1", "u2", "u3", "u4", "attended", "term", "pair", "half",
+             "pieces", "w_qkv", "w_up", "w_out", "w_down", "sems", "loads"]
+    refs = dict(zip(names, refs))
+    refs["units"] = {
+        "qkv": [refs["q0"], refs["q1"], refs["q2"], refs["q3"], refs["w_qkv"], refs["q4"]],
+        "up": [refs["u0"], refs["u1"], refs["u2"], refs["u3"], refs["w_up"], refs["u4"]]}
+    s = Tail(chans, hids, refs)
+    loads = []
+    for i, (src, dst) in enumerate([("wq_hbm", "w_qkv"), ("wu_hbm", "w_up"), ("wo_hbm", "w_out"), ("wd_hbm", "w_down")]):
+        loads.append(pltpu.make_async_copy(refs[src], refs[dst], refs["loads"].at[i]))
+        loads[-1].start()
+    greet(s.rows + s.far + [s.mate])
+    every = range(chunks)
+    for step in (s.scatter, s.collect, s.relay, s.exchange):
+        for t in every:
+            step(t)
+    todo = []
+    for t in every:
+        s.share(t)
+        s.norm(t)
+        if t == 0:
+            loads[0].wait()
+        s.multiply(t, "qkv")
+        s.reduce1(t, "qkv")
+        if t == 0:
+            loads[1].wait()
+        if t:
+            s.reduce2(t - 1, "qkv")
+        s.multiply(t, "up")
+        s.reduce1(t, "up")
+        if t:
+            s.reduce2(t - 1, "up")
+            s.act(t - 1, "qkv")
+            s.act(t - 1, "up")
+            s.gather2(t - 1, "qkv")
+    last = chunks - 1
+    s.reduce2(last, "qkv")
+    s.reduce2(last, "up")
+    if last:
+        s.gather2(last - 1, "up")
+    s.act(last, "qkv")
+    s.act(last, "up")
+    s.gather2(last, "qkv")
+    s.gather2(last, "up")
+    for t in every:
+        s.whole_unit(t, "qkv")
+    s.attend(chunks)
+    loads[2].wait()
+    loads[3].wait()
+    for t in every:
+        s.whole_unit(t, "up")
+        s.down(t)
+        if t:
+            s.total1(t - 1)
+            s.total2(t - 1)
+    s.total1(last)
+    if last:
+        s.total3(last - 1)
+    s.total2(last)
+    s.total3(last)
+    for t in every:
+        s.total4(t)
+    s.drain()
+
+
+def tail(partial, gain, bias, w_qkv, w_up, w_out, w_down, chans, hids, chunks):
+    tok, width = partial.shape
+    rows = tok // chunks
+    size = rows // chans
+    wide = gain.shape[0]
+    chips = hids // 2
+    qw, units = w_qkv.shape[0] * w_qkv.shape[2], w_up.shape[1]
+    bf, vm, hbm = jnp.bfloat16, pl.BlockSpec(memory_space=pltpu.VMEM), pl.BlockSpec(memory_space=pl.ANY)
+    V = pltpu.VMEM
+
+    def unit(w):
+        return [V((chunks, 2, 2, size, w), bf), V((chunks, 2, 2, size, w // 2), bf), V((chunks, 2, size, w // 2), bf),
+                V((chunks, 2, size, w // 2), bf), V((chunks, 2, 2, size, w), bf)]
+
+    few = rows // hids
+    out = pl.pallas_call(
+        functools.partial(tail_kernel, chans, hids, chunks),
+        out_shape=jax.ShapeDtypeStruct((chunks, 2, chips, few, wide), bf),
+        in_specs=[vm] * 3 + [hbm] * 4, out_specs=vm,
+        scratch_shapes=[
+            V((chunks, chans - 1, size, width), bf), V((chunks, hids, size, width), bf), V((chunks, size, HS), jnp.float32),
+            V((chunks, chans, size, HS), jnp.float32), V((chunks, chans, 2, size, width), bf),
+            V((chunks, chans, size, wide), bf), V((chunks, chans, size, wide), bf)]
+        + unit(qw) + unit(units)
+        + [V((tok, w_out.shape[0]), bf), V((chunks, 2, chips, few, wide), bf), V((chunks, chips, few, wide), bf),
+           V((chunks, chips, few, wide), bf), V((chunks, chips - 1, few, wide), bf),
+           V(w_qkv.shape, bf), V(w_up.shape, bf), V(w_out.shape, bf), V(w_down.shape, bf),
+           pltpu.SemaphoreType.DMA((2, 56 * chunks)), pltpu.SemaphoreType.DMA((4,))],
+        compiler_params=pltpu.CompilerParams(collective_id=4, has_side_effects=True, vmem_limit_bytes=60 << 20),
+        name="tail",
+    )(partial.reshape(chunks, chans, size, width), gain.reshape(1, wide), bias.reshape(1, units), w_qkv, w_up, w_out, w_down)
+    return out.reshape(tok, wide)
+
+
 def on_device(
     chans,
     hids,
@@ -361,6 +724,10 @@
     width_hid = patch_weight.shape[2]
     heads_dev = width_hid // HS
     partial_value = pool(pixels.shape[1], pixels, patch_weight, channel_embed, pool_query, group_mix, assign)
+    tile = 16 * max(chans, hids)
+    if chans == 4 and hids == 2 * chans and tok_count % tile == 0:
+        chunks = 2 if tok_count % (2 * tile) == 0 else 1
+        return tail(partial_value, ln_gain, b_up, w_qkv.transpose(1, 0, 2), w_up, w_out, w_down, chans, hids, chunks)
     normed_input, own_cols = layer_rows(partial_value, ln_gain, chans, hids)
     qkv_part = jnp.einsum("td,dke->kte", normed_input, w_qkv, preferred_element_type=jnp.float32)
     up_part = jnp.dot(normed_input, w_up, preferred_element_type=jnp.float32)

time: 197 us -> 161 us (0.82)
  matrix products: 18.6 us -> 0 us
  Pallas kernels: 172 us -> 155 us
    dot_general x6 -> x0, matrix products: 18.6 us -> none  [the longest x1 5.15 us: on_device(): jnp.einsum('td,dke->kte', normed_input, w_qkv, preferred_element_type=jnp...]
    pallas_call x3 -> x1, Pallas kernels: 120 us -> 103 us  [tail(): pl.pallas_call(functools.partial(tail_kernel, chans, hids, chunks), out_s...]
where the time goes in v2:
time: 161 us; the launch traced here: 160 us
  Pallas kernels  155 us (96%)
  local copies, waits for them, and re-layouts  3.35 us (2%)
    pallas_call x1, Pallas kernels, tail(): pl.pallas_call(functools.partial(tail_kernel, chans, hids, chunks), out_s...  103 us
    pallas_call x1, Pallas kernels, pool(): pl.pallas_call(functools.partial(pool_kernel, groups, size), grid_spec=sp...  52.2 us

profile of v2, /device:TPU:25, one launch (start us, length us, event | category | flops | bytes accessed | tf_op | source)
XLA Modules:
  0.0 159.7 jit_solution(2537496613637202472)
XLA Ops:
  0.0 0.7 iota_add_fusion
  0.7 0.2 convert_reduce_fusion
  0.8 0.7 select_reduce_fusion.order
  1.6 1.3 reshape.16.refs_1_
  2.8 52.2 %pool.1 = bf16[256,768]{1,0:T(8,128)(2,1)} custom-call(s32[96]{0:T(128)} %select_reduce_fusion.order, s32[96]{0:T(128)} %assign.1, bf16[96,256,256]{2,1,0:T(8,128)(2,1)} %pix.1, bf16[96,256,768]{2,1,0:T(8,128)(2,1)} %pw.1, bf16[96,768]{1,0:T(8,128)(2,1)} %emb.1, bf16[12,768]{1,0:T(8,128)(2,1)} %query.1, bf16[12,768]{1,0:T(8,128)(2,1)} %mix.1), custom_call_target="tpu_custom_call" | custom-call | tf_op jit(solution)/shard_map/pool/pallas_call | solution.py:139
  55.1 102.6 %tail.1 = bf16[2,2,4,16,1536]{4,3,2,1,0:T(8,128)(2,1)} custom-call(bf16[2,4,32,768]{3,2,1,0:T(8,128)(2,1)} %bitcast.6, f32[1,1536]{1,0:T(1,128)} %reshape.16.refs_1_, f32[1,3072]{1,0:T(1,128)} %bitcast.7, bf16[3,1536,768]{2,1,0:T(8,128)(2,1)} %bitcast.4, bf16[1536,3072]{1,0:T(8,128)(2,1)} %refs_4_.1, bf16[768,1536]{1,0:T(8,128)(2,1)} %refs_5_.1, ...), custom_call_target="tpu_custom_call" | custom-call | tf_op jit(solution)/shard_map/tail/pallas_call | solution.py:688
  157.6 2.1 %copy.14 = bf16[256,1536]{1,0:T(8,128)(2,1)} copy(bf16[256,1536]{1,0:T(8,128)(2,1)} %bitcast.5) | data formatting | bytes 1572864

commit v3 on v2

--- a/solution.py
+++ b/solution.py
@@ -20,20 +20,21 @@
 SLOT = 16
 ROWS = 256
 CPS = 4
+SLOTS = 3
+VMEM_LIMIT = 63 << 20
 
 
 def pool_setup(groups, size, query, mix, emb, quer, pick, shift, mixs, embs, fan):
-    width = quer.shape[1]
+    width = quer.shape[2]
     own = lax.broadcasted_iota(jnp.int32, (SLOT, width), 0) == lax.broadcasted_iota(jnp.int32, (SLOT, width), 1) // HS
     q = query[...].astype(jnp.float32)
     m = mix[...].astype(jnp.float32) * math.sqrt(0.5)
     pick[...] = jnp.where(own, 1.0, 0.0).astype(jnp.bfloat16)
     for g in range(groups):
         row = jnp.where(own, q[g:g+1, :], 0.0)
-        rs = slice(g*SLOT, (g+1)*SLOT)
-        quer[rs, :] = row.astype(jnp.bfloat16)
+        quer[g] = row.astype(jnp.bfloat16)
         n = jnp.sqrt(jnp.sum(row * row, axis=1, keepdims=True)) * LOG2E
-        shift[rs, :] = jnp.broadcast_to(n, (SLOT, HS))
+        shift[g] = jnp.broadcast_to(n, (SLOT, HS))
         mixs[g] = m[g:g+1]
     for c in range(0, emb.shape[0], 8):
         e = emb[c:c+8, :].astype(jnp.float32) * math.sqrt(0.5)
@@ -57,14 +58,22 @@
             put(r, R, cs, g, g * g)
 
 def weigh(tok, g, s, local, quer, pick, shift):
-    rs = pl.ds(pl.multiple_of(local * SLOT, SLOT), SLOT)
-    dots = lax.dot_general(quer[rs, :], g[...], ACROSS, preferred_element_type=jnp.float32)
+    dots = lax.dot_general(quer[local], g[...], ACROSS, preferred_element_type=jnp.float32)
     total = lax.dot_general(pick[...], s[...], ACROSS, preferred_element_type=jnp.float32)
-    sh = jnp.concatenate([shift[rs, :]] * (tok // HS), axis=1)
+    sh = jnp.concatenate([shift[local]] * (tok // HS), axis=1)
     score = dots * lax.rsqrt(total * (1.0 / HS) + 2 * epsilon) * (LOG2E / math.sqrt(HS))
     return jnp.exp2(score - sh)[0:8, :]
 
-def merge(groups, size, tok, order, feat, wts, mixs, fan, acc):
+def weigh_pair(tok, g, s, first, second, quer, pick, shift):
+    query = jnp.concatenate([quer[first], quer[second]], axis=0)
+    dots = lax.dot_general(query, g[...], ACROSS, preferred_element_type=jnp.float32)
+    total = lax.dot_general(pick[...], s[...], ACROSS, preferred_element_type=jnp.float32)[0:8]
+    dots = jnp.concatenate([dots[0:8, :tok], dots[SLOT:SLOT + 8, tok:]], axis=1)
+    sh = jnp.concatenate([shift[first][0:8]] * (tok // HS) + [shift[second][0:8]] * (tok // HS), axis=1)
+    score = dots * lax.rsqrt(total * (1.0 / HS) + 2 * epsilon) * (LOG2E / math.sqrt(HS))
+    return jnp.exp2(score - sh)
+
+def merge(lo, hi, size, tok, order, feat, wts, mixs, fan, acc):
     width = feat.shape[2]
     step = min(256, width)
     def group(g, _):
@@ -88,7 +97,7 @@
                     p = t if p is None else p + t
                 acc[bs, ns] += p * mixs[g, :, ns]
         return 0
-    lax.fori_loop(0, groups, group, 0)
+    lax.fori_loop(lo, hi, group, 0)
 
 def pool_kernel(groups, size, order, assign, pix, pw, emb, query, mix, out, feat, wts, acc, quer, pick, shift, mixs, embs, fan, g0, g1, s0, s1):
     t = pl.program_id(0); c = pl.program_id(1)
@@ -114,7 +123,7 @@
     back(CPS - 1)
     @pl.when(c == pl.num_programs(1)-1)
     def _():
-        merge(groups, size, tok, order, feat, wts, mixs, fan, acc)
+        merge(0, groups, size, tok, order, feat, wts, mixs, fan, acc)
         out[...] = acc[...].astype(jnp.bfloat16)
 
 def pool(T, pixels, patch_weight, channel_embed, pool_query, group_mix, assign):
@@ -133,8 +142,8 @@
           full((chans,width)), full((groups,width)), full((groups,width))],
         out_specs=pl.BlockSpec((T,width), lambda t,c,*_:(t,0)),
         scratch_shapes=[vm((chans,T,width), jnp.bfloat16), vm((chans,8,T), jnp.float32),
-          vm((T,width), jnp.float32), vm((groups*SLOT,width), jnp.bfloat16), vm((SLOT,width), jnp.bfloat16),
-          vm((groups*SLOT,HS), jnp.float32), vm((groups,1,width), jnp.float32), vm((chans,1,width), jnp.float32),
+          vm((T,width), jnp.float32), vm((groups,SLOT,width), jnp.bfloat16), vm((SLOT,width), jnp.bfloat16),
+          vm((groups,SLOT,HS), jnp.float32), vm((groups,1,width), jnp.float32), vm((chans,1,width), jnp.float32),
           vm((size,HS,width), jnp.bfloat16)] + [vm((T,width), jnp.bfloat16)]*4)
     return pl.pallas_call(functools.partial(pool_kernel, groups, size), grid_spec=spec, out_shape=jax.ShapeDtypeStruct((tok,width), jnp.bfloat16),
         compiler_params=pltpu.CompilerParams(dimension_semantics=("arbitrary","arbitrary"), vmem_limit_bytes=62<<20), name="pool")(
@@ -389,10 +398,15 @@
         self.g_near[t] = [self.put(mine, mine, self.mate)]
 
     def relay(self, t):
+        self.c_piece = getattr(self, "c_piece", {})
+        a, chans = self.a, self.chans
         for k in range(1, self.chips):
             self.g_far[t][k - 1].wait_recv()
             piece = self.gath.at[t, lax.rem(self.chip + self.chips - k, self.chips) * 2 + self.core]
             self.g_near[t].append(self.put(piece, piece, self.mate))
+        self.c_piece[t] = [
+            self.put(self.gath.at[t, lax.rem(a + k, chans) * 2 + self.core], self.whole.at[t, a, self.core], self.rows[k - 1])
+            for k in range(1, chans)]
 
     def exchange(self, t):
         for copy in self.g_near[t]:
@@ -408,12 +422,8 @@
         scale = lax.rsqrt(second / (width * self.hids) - mean * mean + epsilon)
         self.stat[t] = jnp.where(lax.broadcasted_iota(jnp.int32, (size, HS), 1) == 0, mean, scale)
         self.c_stat = getattr(self, "c_stat", {})
-        self.c_piece = getattr(self, "c_piece", {})
         a, chans = self.a, self.chans
         self.c_stat[t] = [self.put(self.stat.at[t], self.stats.at[t, a], peer) for peer in self.rows]
-        self.c_piece[t] = [
-            self.put(self.gath.at[t, lax.rem(a + k, chans) * 2 + self.core], self.whole.at[t, a, self.core], self.rows[k - 1])
-            for k in range(1, chans)]
 
     def share(self, t):
         self.c_near = getattr(self, "c_near", {})
@@ -428,11 +438,15 @@
 
         def emit(i, x_of, st):
             for r in range(2):
-                cs = slice(r * width, (r + 1) * width)
-                x = x_of(r)
-                self.own[t, i, :, cs] = x
+                self.own[t, i, :, r * width:(r + 1) * width] = x_of(r)
+
+            def column(n, _):
+                cs = pl.ds(pl.multiple_of(n * HS, HS), HS)
+                x = self.own[t, i, :, cs].astype(jnp.float32)
                 self.normed[t, i, :, cs] = (
-                    (x.astype(jnp.float32) - st[:, 0:1]) * st[:, 1:2] * self.gain[:, cs]).astype(jnp.bfloat16)
+                    (x - st[:, 0:1]) * st[:, 1:2] * self.gain[pl.ds(n, 1), :]).astype(jnp.bfloat16)
+                return 0
+            lax.fori_loop(0, 2 * width // HS, column, 0, unroll=2)
 
         emit(self.a, lambda r: self.gath[t, self.a * 2 + r], self.stat[t])
         for copy in self.c_stat[t] + self.c_near[t]:
@@ -499,7 +513,7 @@
                 v = buf[t, self.y, self.x, :, here].astype(jnp.float32) + got2[t, side, :, cs].astype(jnp.float32)
                 v = v + (got1[t, 0, self.y, :, cs] if side == 0 else got1[t, 1, self.x, :, cs]).astype(jnp.float32)
                 if kind == "up":
-                    v = v + self.bias[:, here]
+                    v = v + self.bias[(base + c) // HS:(base + c) // HS + 1, :]
                     v = (0.5 * v) * (1.0 + lax.erf(v * math.sqrt(0.5)))
                 elif base + c < rotated:
                     v = v * lax.rsqrt(jnp.mean(v * v, axis=-1, keepdims=True) + epsilon)
@@ -520,7 +534,7 @@
         for side in range(2):
             self.e2[t, kind, side].wait_recv()
 
-    def attend(self, chunks):
+    def attend(self, chunks, share, shares):
         full = self.units["qkv"][5]
         size = full.shape[3]
         wide = self.w_qkv.shape[2]
@@ -540,25 +554,42 @@
                 self.attended[rs, pl.ds(pl.multiple_of(h * HS, HS), HS)] = got
             return 0
 
-        lax.fori_loop(0, wide // HS, head, 0)
+        heads = wide // HS
+        lax.fori_loop(heads * share // shares, heads * (share + 1) // shares, head, 0)
+
+    def fetch_down(self):
+        width = self.feat.shape[2]
+        nd, no = self.wd_hbm.shape[0], self.wo_hbm.shape[0]
+        self.down_loads = []
+        for side in range(2):
+            cs = slice(side * width, (side + 1) * width)
+            for hbm, at, count in ((self.wd_hbm, side * nd, nd), (self.wo_hbm, 2 * nd + side * no, no)):
+                copy = pltpu.make_async_copy(hbm.at[:, :, cs], self.feat.at[at:at + count], self.loads.at[2 + len(self.down_loads)])
+                copy.start()
+                self.down_loads.append(copy)
 
     def down(self, t):
         full = self.units["up"][5]
         size = full.shape[3]
         rows = 4 * size
-        wide = self.w_out.shape[1]
-        step = min(256, wide)
+        width = self.feat.shape[2]
+        step = min(256, width)
+        nd, no = self.wd_hbm.shape[0], self.wo_hbm.shape[0]
+        deep = self.feat.shape[1]
         hidden = full[t].reshape(rows, full.shape[4])
         att = self.attended[t * rows:(t + 1) * rows]
 
-        def tile(n, _):
-            cs = pl.ds(pl.multiple_of(n * step, step), step)
-            e = jnp.dot(hidden, self.w_down[:, cs], preferred_element_type=jnp.float32)
-            e = e + jnp.dot(att, self.w_out[:, cs], preferred_element_type=jnp.float32)
-            self.term[t, :, :, :, cs] = e.astype(jnp.bfloat16).reshape(2, self.chips, rows // self.hids, step)
-            return 0
-
-        lax.fori_loop(0, wide // step, tile, 0)
+        for side in range(2):
+            def tile(n, _):
+                off = pl.multiple_of(n * step, step)
+                cs = pl.ds(off, step)
+                wd = self.feat[side * nd:(side + 1) * nd, :, cs].reshape(nd * deep, step)
+                wo = self.feat[2 * nd + side * no:2 * nd + (side + 1) * no, :, cs].reshape(no * deep, step)
+                e = jnp.dot(hidden, wd, preferred_element_type=jnp.float32) + jnp.dot(att, wo, preferred_element_type=jnp.float32)
+                to = pl.ds(pl.multiple_of(side * width + off, step), step)
+                self.term[t, :, :, :, to] = e.astype(jnp.bfloat16).reshape(2, self.chips, rows // self.hids, step)
+                return 0
+            lax.fori_loop(0, width // step, tile, 0)
         self.f1 = getattr(self, "f1", {})
         self.f1[t] = self.put(self.term.at[t, 1 - self.core], self.pair.at[t], self.mate)
 
@@ -603,81 +634,183 @@
             copy.wait_recv()
 
 
-def tail_kernel(chans, hids, chunks, *refs):
-    names = ["part", "gain", "bias", "wq_hbm", "wu_hbm", "wo_hbm", "wd_hbm", "out", "parts", "gath", "stat", "stats", "whole",
-             "own", "normed", "q0", "q1", "q2", "q3", "q4", "u0", "u1", "u2", "u3", "u4", "attended", "term", "pair", "half",
-             "pieces", "w_qkv", "w_up", "w_out", "w_down", "sems", "loads"]
-    refs = dict(zip(names, refs))
-    refs["units"] = {
-        "qkv": [refs["q0"], refs["q1"], refs["q2"], refs["q3"], refs["w_qkv"], refs["q4"]],
-        "up": [refs["u0"], refs["u1"], refs["u2"], refs["u3"], refs["w_up"], refs["u4"]]}
-    s = Tail(chans, hids, refs)
-    loads = []
-    for i, (src, dst) in enumerate([("wq_hbm", "w_qkv"), ("wu_hbm", "w_up"), ("wo_hbm", "w_out"), ("wd_hbm", "w_down")]):
-        loads.append(pltpu.make_async_copy(refs[src], refs[dst], refs["loads"].at[i]))
-        loads[-1].start()
-    greet(s.rows + s.far + [s.mate])
-    every = range(chunks)
-    for step in (s.scatter, s.collect, s.relay, s.exchange):
-        for t in every:
-            step(t)
-    todo = []
-    for t in every:
-        s.share(t)
-        s.norm(t)
+NAMES = [
+    "order", "assign", "emb", "query", "mix", "gain", "bias", "pix_hbm", "pw_hbm", "wq_hbm", "wu_hbm", "wo_hbm", "wd_hbm", "out",
+    "part", "parts", "gath", "stat", "stats", "whole", "own", "normed", "q0", "q1", "q2", "q3", "q4", "u0",
+    "u1", "u2", "u3", "u4", "attended", "term", "pair", "half", "pieces", "w_qkv", "w_up", "feat", "wts", "acc",
+    "quer", "pick", "shift", "mixs", "embs", "fan", "g0", "g1", "s0", "s1", "pix", "pw", "sems", "loads",
+    "fetches",
+]
+
+
+def block_kernel(chans, hids, chunks, groups, *refs):
+    r = dict(zip(NAMES, refs))
+    r["units"] = {
+        "qkv": [r["q0"], r["q1"], r["q2"], r["q3"], r["w_qkv"], r["q4"]],
+        "up": [r["u0"], r["u1"], r["u2"], r["u3"], r["w_up"], r["u4"]]}
+    s = Tail(chans, hids, r)
+    count, tok = s.feat.shape[:2]
+    size = count // groups
+    slots, per = s.pix.shape[:2]
+    blocks = count // per
+    ahead = slots - 1
+    gb, sb = (s.g0, s.g1), (s.s0, s.s1)
+
+    def fetch(t, i):
+        slot = lax.rem(t * blocks + i, slots)
+        cs = pl.ds(i * per, per)
+        return (pltpu.make_async_copy(s.pw_hbm.at[cs], s.pw.at[slot], s.fetches.at[0, slot]),
+                pltpu.make_async_copy(s.pix_hbm.at[cs, t * tok:(t + 1) * tok], s.pix.at[slot], s.fetches.at[1, slot]))
+
+    def start(t, i):
+        for copy in fetch(t, i):
+            copy.start()
+
+    def back(cc, pair):
+        w = weigh_pair(tok, gb[pair], sb[pair], s.assign[cc], s.assign[cc + 1], s.quer, s.pick, s.shift)
+        s.wts[cc] = w[:, :tok]
+        s.wts[cc + 1] = w[:, tok:]
+
+    def embed(t, lo, hi):
+        def block(i, _):
+            @pl.when(i + ahead < blocks)
+            def _():
+                start(t, i + ahead)
+            if t + 1 < chunks:
+                @pl.when(i + ahead >= blocks)
+                def _():
+                    start(t + 1, i + ahead - blocks)
+            for copy in fetch(t, i):
+                copy.wait()
+            slot = lax.rem(t * blocks + i, slots)
+
+            for k in range(per):
+                cc = i * per + k
+                pair = k // 2 % 2
+                def keep(rr, R, cs, g, sq):
+                    s.feat[cc, rr:rr+R, cs] = g
+                    at = k % 2 * tok + rr
+                    gb[pair][at:at+R, cs] = g
+                    sb[pair][at:at+R, cs] = sq
+                features(tok, lambda rr, R: s.pix[slot, k, rr:rr+R, :], lambda cs: s.pw[slot, k, :, cs], s.embs[cc], keep)
+                if k % 2:
+                    back(jnp.maximum(cc - 3, 0), 1 - pair)
+            return 0
+        lax.fori_loop(lo, hi, block, 0)
+        if hi == blocks:
+            back(count - 2, 1)
+
+    def mix_in(t, lo, hi):
+        if lo == 0:
+            s.acc[...] = jnp.zeros_like(s.acc)
+        merge(lo, hi, size, tok, s.order, s.feat, s.wts, s.mixs, s.fan, s.acc)
+        if hi == groups:
+            s.part[t] = s.acc[...].astype(jnp.bfloat16).reshape(s.part.shape[1:])
+
+    gate = pltpu.get_barrier_semaphore()
+    peers = s.rows + s.far + [s.mate]
+    for peer in peers:
+        pl.semaphore_signal(gate, inc=1, device_id=peer, device_id_type=MESH)
+    for i in range(ahead):
+        start(0, i)
+    loads = [pltpu.make_async_copy(s.wq_hbm, s.w_qkv, s.loads.at[0]), pltpu.make_async_copy(s.wu_hbm, s.w_up, s.loads.at[1])]
+    pool_setup(groups, size, s.query, s.mix, s.emb, s.quer, s.pick, s.shift, s.mixs, s.embs, s.fan)
+    embed(0, 0, blocks // 3)
+    loads[0].start()
+    embed(0, blocks // 3, 2 * blocks // 3)
+    loads[1].start()
+    embed(0, 2 * blocks // 3, blocks)
+    mix_in(0, 0, groups)
+    pl.semaphore_wait(gate, len(peers))
+    s.scatter(0)
+
+    def front(t):
         if t == 0:
             loads[0].wait()
+        s.norm(t)
         s.multiply(t, "qkv")
         s.reduce1(t, "qkv")
         if t == 0:
             loads[1].wait()
-        if t:
-            s.reduce2(t - 1, "qkv")
         s.multiply(t, "up")
         s.reduce1(t, "up")
-        if t:
-            s.reduce2(t - 1, "up")
-            s.act(t - 1, "qkv")
-            s.act(t - 1, "up")
-            s.gather2(t - 1, "qkv")
+
+    for t in range(1, chunks):
+        u = t - 1
+        steps = [(4, lambda: s.collect(u)), (9, lambda: s.relay(u)), (11, lambda: s.exchange(u)), (13, lambda: s.share(u)),
+                 (15, lambda: front(u)), (19, lambda: s.reduce2(u, "qkv")), (22, lambda: s.reduce2(u, "up"))]
+        at = 0
+        for mark, step in steps:
+            mark = min(blocks, mark * blocks // 24)
+            if mark > at:
+                embed(t, at, mark)
+            at = mark
+            step()
+        if at < blocks:
+            embed(t, at, blocks)
+        cuts = [groups * k // 4 for k in range(5)]
+        mix_in(t, cuts[0], cuts[1])
+        s.act(u, "qkv")
+        mix_in(t, cuts[1], cuts[2])
+        s.act(u, "up")
+        mix_in(t, cuts[2], cuts[3])
+        s.gather2(u, "qkv")
+        mix_in(t, cuts[3], cuts[4])
+        s.scatter(t)
+        s.gather2(u, "up")
+    s.fetch_down()
     last = chunks - 1
+    s.collect(last)
+    s.relay(last)
+    s.exchange(last)
+    s.share(last)
+    front(last)
     s.reduce2(last, "qkv")
+    s.act(last, "qkv")
     s.reduce2(last, "up")
-    if last:
-        s.gather2(last - 1, "up")
-    s.act(last, "qkv")
+    s.gather2(last, "qkv")
     s.act(last, "up")
-    s.gather2(last, "qkv")
-    s.gather2(last, "up")
+    every = range(chunks)
     for t in every:
         s.whole_unit(t, "qkv")
-    s.attend(chunks)
-    loads[2].wait()
-    loads[3].wait()
+    s.attend(chunks, 0, 3)
+    s.gather2(last, "up")
+    s.attend(chunks, 1, 3)
+    s.attend(chunks, 2, 3)
+    for copy in s.down_loads:
+        copy.wait()
     for t in every:
         s.whole_unit(t, "up")
-        s.down(t)
         if t:
             s.total1(t - 1)
-            s.total2(t - 1)
+        s.down(t)
     s.total1(last)
-    if last:
-        s.total3(last - 1)
-    s.total2(last)
-    s.total3(last)
-    for t in every:
-        s.total4(t)
+    for step in (s.total2, s.total3, s.total4):
+        for t in every:
+            step(t)
     s.drain()
 
 
-def tail(partial, gain, bias, w_qkv, w_up, w_out, w_down, chans, hids, chunks):
-    tok, width = partial.shape
+def sort_channels(assign):
+    chans = assign.shape[0]
+    idx = jnp.arange(chans, dtype=jnp.int32)
+    key = assign * chans + idx
+    rank = jnp.sum((key[None, :] < key[:, None]).astype(jnp.int32), axis=1)
+    return jnp.sum(jnp.where(rank[None, :] == idx[:, None], idx[None, :], 0), axis=1).astype(jnp.int32)
+
+
+def block(pixels, patch_weight, channel_embed, pool_query, group_mix, assign, gain, bias, w_qkv, w_up, w_out, w_down, chans, hids, chunks):
+    count, tok, p2 = pixels.shape
+    width = patch_weight.shape[2]
+    groups = pool_query.shape[0]
     rows = tok // chunks
     size = rows // chans
     wide = gain.shape[0]
     chips = hids // 2
     qw, units = w_qkv.shape[0] * w_qkv.shape[2], w_up.shape[1]
-    bf, vm, hbm = jnp.bfloat16, pl.BlockSpec(memory_space=pltpu.VMEM), pl.BlockSpec(memory_space=pl.ANY)
+    bf, f32 = jnp.bfloat16, jnp.float32
+    sm = pl.BlockSpec(memory_space=pltpu.SMEM)
+    vm, hbm = pl.BlockSpec(memory_space=pltpu.VMEM), pl.BlockSpec(memory_space=pl.ANY)
     V = pltpu.VMEM
 
     def unit(w):
@@ -686,21 +819,28 @@
 
     few = rows // hids
     out = pl.pallas_call(
-        functools.partial(tail_kernel, chans, hids, chunks),
+        functools.partial(block_kernel, chans, hids, chunks, groups),
         out_shape=jax.ShapeDtypeStruct((chunks, 2, chips, few, wide), bf),
-        in_specs=[vm] * 3 + [hbm] * 4, out_specs=vm,
+        in_specs=[sm] * 2 + [vm] * 5 + [hbm] * 6, out_specs=vm,
         scratch_shapes=[
-            V((chunks, chans - 1, size, width), bf), V((chunks, hids, size, width), bf), V((chunks, size, HS), jnp.float32),
-            V((chunks, chans, size, HS), jnp.float32), V((chunks, chans, 2, size, width), bf),
+            V((chunks, chans, size, width), bf),
+            V((chunks, chans - 1, size, width), bf), V((chunks, hids, size, width), bf), V((chunks, size, HS), f32),
+            V((chunks, chans, size, HS), f32), V((chunks, chans, 2, size, width), bf),
             V((chunks, chans, size, wide), bf), V((chunks, chans, size, wide), bf)]
         + unit(qw) + unit(units)
         + [V((tok, w_out.shape[0]), bf), V((chunks, 2, chips, few, wide), bf), V((chunks, chips, few, wide), bf),
            V((chunks, chips, few, wide), bf), V((chunks, chips - 1, few, wide), bf),
-           V(w_qkv.shape, bf), V(w_up.shape, bf), V(w_out.shape, bf), V(w_down.shape, bf),
-           pltpu.SemaphoreType.DMA((2, 56 * chunks)), pltpu.SemaphoreType.DMA((4,))],
-        compiler_params=pltpu.CompilerParams(collective_id=4, has_side_effects=True, vmem_limit_bytes=60 << 20),
-        name="tail",
-    )(partial.reshape(chunks, chans, size, width), gain.reshape(1, wide), bias.reshape(1, units), w_qkv, w_up, w_out, w_down)
+           V(w_qkv.shape, bf), V(w_up.shape, bf),
+           V((count, rows, width), bf), V((count, 8, rows), f32), V((rows, width), f32),
+           V((groups, SLOT, width), bf), V((SLOT, width), bf), V((groups, SLOT, HS), f32),
+           V((groups, 1, width), f32), V((count, 1, width), f32), V((count // groups, HS, width), bf)]
+        + [V((2 * rows, width), bf)] * 4
+        + [V((SLOTS, CPS, rows, p2), bf), V((SLOTS, CPS, p2, width), bf),
+           pltpu.SemaphoreType.DMA((2, 48 * chunks)), pltpu.SemaphoreType.DMA((6,)), pltpu.SemaphoreType.DMA((2, SLOTS))],
+        compiler_params=pltpu.CompilerParams(collective_id=4, has_side_effects=True, vmem_limit_bytes=VMEM_LIMIT),
+        name="block",
+    )(sort_channels(assign), lax.rem(assign, groups), channel_embed, pool_query, group_mix, gain.reshape(wide // HS, HS), bias.reshape(units // HS, HS),
+      pixels, patch_weight, w_qkv, w_up, w_out.reshape(w_out.shape[0] // rows, rows, wide), w_down.reshape(units // rows, rows, wide))
     return out.reshape(tok, wide)
 
 
@@ -723,11 +863,15 @@
     tok_count = pixels.shape[1]
     width_hid = patch_weight.shape[2]
     heads_dev = width_hid // HS
-    partial_value = pool(pixels.shape[1], pixels, patch_weight, channel_embed, pool_query, group_mix, assign)
     tile = 16 * max(chans, hids)
-    if chans == 4 and hids == 2 * chans and tok_count % tile == 0:
-        chunks = 2 if tok_count % (2 * tile) == 0 else 1
-        return tail(partial_value, ln_gain, b_up, w_qkv.transpose(1, 0, 2), w_up, w_out, w_down, chans, hids, chunks)
+    chunks = 2 if tok_count % (2 * tile) == 0 else 1
+    rows = tok_count // chunks
+    units = w_up.shape[1]
+    room = 2 * (units + width_hid) <= pixels.shape[0] * rows
+    if chans == 4 and hids == 2 * chans and tok_count % tile == 0 and rows % HS == 0 and units % rows == 0 and width_hid % rows == 0 and room:
+        return block(pixels, patch_weight, channel_embed, pool_query, group_mix, assign, ln_gain, b_up,
+                     w_qkv.transpose(1, 0, 2), w_up, w_out, w_down, chans, hids, chunks)
+    partial_value = pool(tok_count, pixels, patch_weight, channel_embed, pool_query, group_mix, assign)
     normed_input, own_cols = layer_rows(partial_value, ln_gain, chans, hids)
     qkv_part = jnp.einsum("td,dke->kte", normed_input, w_qkv, preferred_element_type=jnp.float32)
     up_part = jnp.dot(normed_input, w_up, preferred_element_type=jnp.float32)

time: 161 us -> 151 us (0.938)
  Pallas kernels: 155 us -> 145 us
    pallas_call x2 -> x1, Pallas kernels: 155 us -> 145 us  [block(): pl.pallas_call(functools.partial(block_kernel, chans, hids, chunks, group...]
where the time goes in v3:
time: 151 us; the launch traced here: 150 us
  Pallas kernels  145 us (96%)
  local copies, waits for them, and re-layouts  2.06 us (1%)
  other arithmetic  2.04 us (1%)
    pallas_call x1, Pallas kernels, block(): pl.pallas_call(functools.partial(block_kernel, chans, hids, chunks, group...  145 us

profile of v3, /device:TPU:25, one launch (start us, length us, event | category | flops | bytes accessed | tf_op | source)
XLA Modules:
  0.0 149.5 jit_solution(12948022456041145783)
XLA Ops:
  0.0 1.2 broadcast_remainder_fusion
  1.2 0.2 convert_reduce_fusion
  1.3 0.7 select_reduce_fusion.refs_0_
  2.1 145.4 %block.1 = bf16[2,2,4,16,1536]{4,3,2,1,0:T(8,128)(2,1)} custom-call(s32[96]{0:T(128)} %select_reduce_fusion.refs_0_, s32[96]{0:T(128)} %get-tuple-element.5.refs_1_, bf16[96,768]{1,0:T(8,128)(2,1)} %refs_2_.1, bf16[12,768]{1,0:T(8,128)(2,1)} %refs_3_.1, bf16[12,768]{1,0:T(8,128)(2,1)} %refs_4_.1, f32[12,128]{1,0:T(8,128)} %bitcast.11, f32[24,128]{1,0:T(8,128)} %bitcast.10, ...), custom_call_target="tpu_custom_call" | custom-call | tf_op jit(solution)/shard_map/block/pallas_call | solution.py:821
  147.4 2.1 %copy.14 = bf16[256,1536]{1,0:T(8,128)(2,1)} copy(bf16[256,1536]{1,0:T(8,128)(2,1)} %bitcast.8) | data formatting | bytes 1572864
